TPU v7x, 512 devices: a whole 4x4x16 slice. The times are simulated.
512 devices in a mesh: band: 8 (over y, core), pw: 64 (over z, x).
Axes of the slice: x: 4, y: 4, z: 16, core: 2. Of those that a mesh axis runs over, the one named last changes fastest.
Arguments:
- occupied_bands: float32 [2, 16, 3328, 128], P(None, 'band', 'pw'), may hold values from -0.11742834 to 0.11742834
- iterate: float32 [2, 16, 3328, 128], P(None, 'band', 'pw'), may hold values from -2 to 2
- residual: float32 [2, 16, 3328, 128], P(None, 'band', 'pw'), may hold values from -25 to 25, as said below
- old_direction: float32 [2, 16, 3328, 128], P(None, 'band', 'pw'), may hold values from -25 to 25, as said below
- preconditioner: float32 [16, 3328, 128], P('band', 'pw'), may hold values from 0.1 to 1
- old_norm: float32 [16], P('band'), may hold values from 0.4 to 1.6
- eigenvalues: float32 [16], replicated, may hold values from -2 to -0.3
- band_slot: int32 [16], replicated, may hold values from 0 to 15, each once
- potential: float32 [128, 128, 128], P('pw'), may hold values from 0.2 to 1.5
- column_map: int32 [3328], replicated, may hold values from 0 to 16383, as said below
Outputs:
- new_iterate: float32 [2, 16, 3328, 128], P(None, 'band', 'pw')
- new_residual: float32 [2, 16, 3328, 128], P(None, 'band', 'pw')
- direction: float32 [2, 16, 3328, 128], P(None, 'band', 'pw')
- new_norm: float32 [16], P('band')
- density: float32 [128, 128, 128], P('pw', 'band')
Inputs may be any that keep to these rules, and one draw needn't show every extreme that they name: `residual`: random draw per entry, rough from column to column and frequency to frequency. `old_direction`: random draw per entry, rough from column to column and frequency to frequency. `column_map`: distinct flat indices; every column with signed a^2 + b^2 < 32^2 is present, the remaining columns lie outside that disc; the column of flat index 0 is present. `band_slot`: each global band index appears once.
All inputs are finite; a program needn't handle non-finite values.
Results may differ from a plain program's by a relative error of at most 0.0001.
Values sent between devices are 32-bit elements; how exact they have to be, the bound alone decides.
A program may use at most 64 MiB of HBM per device.

v0:
```python
import math

import jax
import jax.numpy as jnp
from jax import lax
from jax.sharding import PartitionSpec as P

exact_mode = lax.Precision.HIGHEST


def phase_table(grid_len, direction_sign):
    indices = jnp.arange(grid_len, dtype=jnp.int32)
    phases = indices[:, None] * indices[None, :] % grid_len
    angles = phases.astype(jnp.float32) * (2.0 * math.pi / grid_len)
    cosine = jnp.cos(angles)
    sine_part = jnp.sin(angles) * direction_sign
    return jnp.stack([jnp.stack([cosine, sine_part]), jnp.stack([-sine_part, cosine])])


def signed_index(values, grid_len):
    return jnp.where(values < grid_len // 2, values, values - grid_len)


def wave_squares(columns, grid_len):
    wave_x = signed_index(columns // grid_len, grid_len)
    wave_y = signed_index(columns % grid_len, grid_len)
    wave_z = signed_index(jnp.arange(grid_len, dtype=jnp.int32), grid_len)
    return (wave_x * wave_x + wave_y * wave_y)[:, None] + (wave_z * wave_z)[None, :]


def correlation(band_rows, vectors):
    real_part = jnp.einsum("pvck,pnck->vn", band_rows, vectors, precision=exact_mode)
    imag_part = jnp.einsum(
        "vck,nck->vn", band_rows[0], vectors[1], precision=exact_mode
    ) - jnp.einsum("vck,nck->vn", band_rows[1], vectors[0], precision=exact_mode)
    return jnp.stack([real_part, imag_part])


def expand(band_rows, weights):
    real_part = jnp.einsum(
        "vck,vn->nck", band_rows[0], weights[0], precision=exact_mode
    ) - jnp.einsum("vck,vn->nck", band_rows[1], weights[1], precision=exact_mode)
    imag_part = jnp.einsum(
        "vck,vn->nck", band_rows[0], weights[1], precision=exact_mode
    ) + jnp.einsum("vck,vn->nck", band_rows[1], weights[0], precision=exact_mode)
    return jnp.stack([real_part, imag_part])


def column_transform(coefficients, phase_grid):
    mixed_cols = jnp.einsum("pbck,pqkz->qbzc", coefficients, phase_grid, precision=exact_mode)
    return lax.all_to_all(mixed_cols, "pw", split_axis=2, concat_axis=3, tiled=True)


def to_grid(columns, inverse_map, phase_grid, grid_len):
    item_rows = columns.shape[1]
    col_count = columns.shape[2]
    rows_first = columns.reshape(2 * item_rows, col_count).T
    padded = jnp.concatenate([rows_first, jnp.zeros((1, 2 * item_rows), jnp.float32)], axis=0)
    placed = jnp.take(padded, inverse_map, axis=0)
    field_grid = placed.T.reshape(2, item_rows, grid_len, grid_len)
    field_grid = jnp.einsum("pzxk,pqky->qzxy", field_grid, phase_grid, precision=exact_mode)
    return jnp.einsum("pzky,pqkx->qzxy", field_grid, phase_grid, precision=exact_mode)


def from_grid(field_grid, column_map, phase_grid, grid_len):
    item_rows = field_grid.shape[1]
    field_grid = jnp.einsum("pzxk,pqky->qzxy", field_grid, phase_grid, precision=exact_mode)
    field_grid = jnp.einsum("pzky,pqkx->qzxy", field_grid, phase_grid, precision=exact_mode)
    cells_first = field_grid.reshape(2 * item_rows, grid_len * grid_len).T
    picked = jnp.take(cells_first, column_map, axis=0)
    return picked.T.reshape(2, item_rows, column_map.shape[0])


def on_device(
    occupied_bands,
    iterate,
    residual,
    old_direction,
    preconditioner,
    old_norm,
    eigenvalues,
    band_slot,
    potential,
    column_map,
):
    grid_len = potential.shape[1]
    planes = potential.shape[0]
    local_bands = iterate.shape[1]
    local_cols = iterate.shape[2]
    col_count = column_map.shape[0]
    total_pw = col_count * grid_len
    forward_table = phase_table(grid_len, 1.0)
    inverse_table = phase_table(grid_len, -1.0)
    inverse_map = (
        jnp.full((grid_len * grid_len,), col_count, jnp.int32)
        .at[column_map]
        .set(jnp.arange(col_count, dtype=jnp.int32))
    )
    my_columns = lax.dynamic_slice_in_dim(column_map, lax.axis_index("pw") * local_cols, local_cols)
    squares = wave_squares(my_columns, grid_len)
    kinetic = squares.astype(jnp.float32) * (4.0 / (grid_len * grid_len))
    sphere = (squares < grid_len // 4 * (grid_len // 4)).astype(jnp.float32)
    occupied = occupied_bands * sphere
    start_wave = iterate * sphere
    masked_residual = residual * sphere
    previous = old_direction * sphere
    weight = preconditioner * sphere
    owner_ids = lax.dynamic_slice_in_dim(
        band_slot, lax.axis_index("band") * local_bands, local_bands
    )
    select = (
        owner_ids[:, None] == jnp.arange(band_slot.shape[0], dtype=jnp.int32)[None, :]
    ).astype(jnp.float32)
    band_energy = jnp.dot(select, eigenvalues, precision=exact_mode)
    all_occupied = lax.all_gather(occupied_bands, "band", axis=1, tiled=True) * sphere
    smoothed = weight[None] * masked_residual
    norm_local = (
        jnp.sum(weight[None] * masked_residual * masked_residual, axis=(0, 2, 3)) / total_pw
    )
    new_norm = lax.psum(norm_local, "pw")
    beta_ratio = new_norm / old_norm
    direction = smoothed + beta_ratio[None, :, None, None] * previous
    weights = lax.psum(correlation(all_occupied, direction), "pw")
    projected = expand(all_occupied, weights)
    direction_cols = column_transform(direction, forward_table)
    field_grid = to_grid(
        direction_cols.reshape(2, local_bands * planes, -1), inverse_map, forward_table, grid_len
    )
    field_grid = (
        field_grid.reshape(2, local_bands, planes, grid_len, grid_len) * potential[None, None]
    ).reshape(2, local_bands * planes, grid_len, grid_len)
    returned = from_grid(field_grid, column_map, inverse_table, grid_len)
    gathered_back = lax.all_to_all(
        returned.reshape(2, local_bands, planes, -1), "pw", split_axis=3, concat_axis=2, tiled=True
    )
    local_potential = jnp.einsum(
        "pbzc,pqzk->qbck", gathered_back, inverse_table, precision=exact_mode
    ) / float(grid_len**3)
    applied = (
        local_potential * sphere
        + (kinetic[None, None] - band_energy[None, :, None, None]) * direction
        + projected
    )
    curvature_local = jnp.sum(direction * applied, axis=(0, 2, 3)) / total_pw
    curvature = lax.psum(curvature_local, "pw")
    step_size = new_norm / curvature
    new_iterate = start_wave + step_size[None, :, None, None] * direction
    new_residual = masked_residual - step_size[None, :, None, None] * applied
    joined = column_transform(jnp.concatenate([occupied, new_iterate], axis=1), forward_table)
    both_grids = to_grid(
        joined.reshape(2, 2 * local_bands * planes, -1), inverse_map, forward_table, grid_len
    )
    both_grids = both_grids.reshape(2, 2, local_bands, planes, grid_len, grid_len)
    density_local = jnp.sum(both_grids[:, 0] * both_grids[:, 1], axis=(0, 1)) * (4.0 / total_pw)
    density = lax.psum_scatter(density_local, "band", scatter_dimension=1, tiled=True)
    return (new_iterate, new_residual, direction, new_norm, density)


def solution(mesh):
    in_specs = (
        P(None, "band", "pw", None),
        P(None, "band", "pw", None),
        P(None, "band", "pw", None),
        P(None, "band", "pw", None),
        P("band", "pw", None),
        P("band"),
        P(),
        P(),
        P("pw", None, None),
        P(),
    )
    out_specs = (
        P(None, "band", "pw", None),
        P(None, "band", "pw", None),
        P(None, "band", "pw", None),
        P("band"),
        P("pw", "band", None),
    )
    return jax.shard_map(
        on_device, mesh=mesh, in_specs=in_specs, out_specs=out_specs, check_vma=False
    )
```

profile of v0, /device:TPU:1, one launch (start us, length us, event | category | flops | bytes accessed | tf_op | source)
XLA Modules:
  0.0 810.4 jit_solution(9233818517082111334)
XLA Ops:
  11.4 122.6 %psum.21 = f32[2]{0:T(128)S(1)} all-reduce(f32[2]{0:T(128)S(1)} %broadcast_multiply_fusion.4), channel_id=1, replica_groups=mesh['band'=8,'pw'=64] {'pw'}, use_global_device_ids=true, to_apply=%region_1.2 | all-reduce | flops 2 | bytes 16 | tf_op jit(solution)/shard_map/psum | solution.py:120
  138.9 6.7 all-to-all-start
  148.0 42.5 %all_gather.3 = f32[2,16,52,128]{3,0,2,1:T(2,128)S(1)} all-gather(f32[2,2,52,128]{3,0,2,1:T(2,128)S(1)} %copy.102), channel_id=1, replica_groups=mesh['band'=8,'pw'=64] {'band'}, dimensions={1}, use_global_device_ids=true | all-gather | bytes 958464 | tf_op jit(solution)/shard_map/all_gather | solution.py:115
  193.1 115.7 %psum.22 = f32[2,16,2]{1,2,0:T(2,128)S(1)} all-reduce(f32[2,16,2]{1,2,0:T(2,128)S(1)} %pad_maximum_fusion.12), channel_id=1, replica_groups=mesh['band'=8,'pw'=64] {'pw'}, use_global_device_ids=true, to_apply=%region_3.4 | all-reduce | flops 64 | bytes 512 | tf_op jit(solution)/shard_map/psum | solution.py:123
  313.9 12.7 %scatter_custom_fusion = s32[16384]{0:T(1024)S(1)} fusion(s32[3328]{0:T(1024)S(1)} %compare_select_fusion.1, s32[3328]{0:T(1024)S(1)} %iota.54, s32[]{:T(128)} %constant.107.clone.1), kind=kCustom, calls=%fused_computation.104 | custom fusion | bytes 65540 | tf_op jit(solution)/shard_map/scatter | solution.py:97
  331.1 60.2 %gather_fusion = f32[16384,8]{1,0:T(8,128)} fusion(f32[3329,8]{1,0:T(8,128)S(1)} %concatenate.9, s32[16384]{0:T(1024)} %fusion.49), kind=kCustom, calls=%fused_computation | custom fusion | bytes 1114112 | tf_op jit(solution)/shard_map/jit(_take)/gather | solution.py:59
  391.3 13.1 %select_bitcast_fusion.1 = f32[8,16384]{0,1:T(8,128)} fusion(f32[16384,8]{1,0:T(8,128)} %gather_fusion, pred[16384]{0:T(1024)(128)(4,1)S(1)} %copy-done.24), kind=kLoop, calls=%fused_computation.5 | loop fusion | flops 131072 | bytes 1064960 | tf_op jit(solution)/shard_map/jit(_take)/select_n | solution.py:59
  404.4 5.6 copy.86
  414.9 5.3 copy.95
  420.1 8.8 %gather_fusion.1 = f32[3328,8]{1,0:T(8,128)S(1)} fusion(f32[16384,8]{1,0:T(8,128)} %bitcast.224, s32[4096]{0:T(1024)S(1)} %copy-done.30), kind=kCustom, calls=%fused_computation.1 | custom fusion | bytes 226304 | tf_op jit(solution)/shard_map/jit(_take)/gather | solution.py:70
  430.8 6.6 reshape.309
  437.4 10.1 %reshape.314 = f32[64,1,416]{2,1,0:T(1,128)} reshape(f32[3328,2,2,2]{3,2,1,0:T(2,128)} %bitcast.226) | data formatting | bytes 212992
  447.5 10.0 %all-to-all-start.1 = ((f32[64,1,416]{2,1,0:T(1,128)}), f32[64,1,416]{2,1,0:T(1,128)S(1)}, u32[]{:S(2)}, u32[]{:S(2)}) async-start(f32[64,1,416]{2,1,0:T(1,128)} %reshape.314), calls=%async_computation.1 | async-start | bytes 262144 | tf_op jit(solution)/shard_map/all_to_all | solution.py:133
  457.8 14.8 %all-to-all-done.1 = f32[64,1,416]{2,1,0:T(1,128)S(1)} async-done(((f32[64,1,416]{2,1,0:T(1,128)}), f32[64,1,416]{2,1,0:T(1,128)S(1)}, u32[]{:S(2)}, u32[]{:S(2)}) %all-to-all-start.1) | async-done | bytes 106528 | tf_op jit(solution)/shard_map/all_to_all | solution.py:133
  473.5 11.8 %reshape.315 = f32[3328,2,2,2]{3,2,1,0:T(2,128)} reshape(f32[64,416]{1,0:T(8,128)S(1)} %reduce.2) | data formatting | bytes 212992
  485.3 10.3 %copy.165 = f32[2,2,2,64,52]{4,3,2,1,0:T(8,128)S(1)} copy(f32[2,2,2,64,52]{2,1,0,4,3:T(2,128)} %bitcast.225) | data formatting | bytes 212992 | tf_op jit(solution)/shard_map/all_to_all | solution.py:133
  496.5 111.4 %psum.23 = f32[2]{0:T(128)S(1)} all-reduce(f32[2]{0:T(128)S(1)} %broadcast_multiply_fusion.3), channel_id=1, replica_groups=mesh['band'=8,'pw'=64] {'pw'}, use_global_device_ids=true, to_apply=%region_5.6 | all-reduce | flops 2 | bytes 16 | tf_op jit(solution)/shard_map/psum | solution.py:145
  610.9 21.6 %all_to_all.48 = f32[64,1,832]{2,1,0:T(1,128)S(1)} all-to-all(f32[64,1,832]{2,1,0:T(1,128)S(1)} %reshape.316), channel_id=1, replica_groups=mesh['band'=8,'pw'=64] {'pw'}, dimensions={0} | all-to-all | bytes 425984 | tf_op jit(solution)/shard_map/all_to_all | solution.py:51
  635.7 60.0 %gather_fusion.2 = f32[16384,16]{1,0:T(8,128)} fusion(f32[3329,16]{1,0:T(8,128)S(1)} %concatenate.11, s32[16384]{0:T(1024)} %fusion.49), kind=kCustom, calls=%fused_computation.2 | custom fusion | bytes 2162688 | tf_op jit(solution)/shard_map/jit(_take)/gather | solution.py:59
  695.7 13.2 %select_bitcast_fusion = f32[16,16384]{0,1:T(8,128)} fusion(f32[16384,16]{1,0:T(8,128)} %gather_fusion.2, pred[16384]{0:T(1024)(128)(4,1)S(1)} %copy-done.25), kind=kLoop, calls=%fused_computation.4 | loop fusion | flops 262144 | bytes 2113536 | tf_op jit(solution)/shard_map/jit(_take)/select_n | solution.py:59
  708.9 5.2 copy.118
  714.0 2.0 convolution_bitcast_fusion
  716.0 1.9 fusion.20
  720.8 82.8 %reduce-scatter.2.cloned.1.call-done = f32[2,16,128]{2,1,0:T(8,128)} async-done(((f32[2,128,128]{2,1,0:T(8,128)}), f32[2,16,128]{2,1,0:T(8,128)}) %reduce-scatter.2.cloned.1.call-update) | async-done | bytes 16400 | tf_op jit(solution)/shard_map/reduce_scatter | solution.py:155
  (146 shorter events, 41.0 us)
Async XLA Ops:
  7.2 320.2 %copy-start = (f32[16]{0:T(128)S(1)}, f32[16]{0:T(128)}, u32[]{:S(2)}) copy-start(f32[16]{0:T(128)} %param.16) | copy-start | bytes 196
  7.2 320.1 %copy-start.31 = (s32[16]{0:T(128)S(1)}, s32[16]{0:T(128)}, u32[]{:S(2)}) copy-start(s32[16]{0:T(128)} %param.17) | copy-start | bytes 196
  8.6 321.7 %copy-start.13 = (f32[52,128]{1,0:T(8,128)}, f32[52,128]{1,0:T(8,128)S(1)}, u32[]{:S(2)}) copy-start(f32[52,128]{1,0:T(8,128)S(1)} %fusion.58) | copy-start | bytes 79876
  135.7 195.3 %copy-start.6 = (f32[2,2,52,128]{3,2,1,0:T(8,128)}, f32[2,2,52,128]{3,2,1,0:T(8,128)S(1)}, u32[]{:S(2)}) copy-start(f32[2,2,52,128]{3,2,1,0:T(8,128)S(1)} %multiply_add_fusion) | copy-start | bytes 319492
  138.9 189.3 %all-to-all-start = ((f32[64,1,416]{2,1,0:T(1,128)}), f32[64,1,416]{2,1,0:T(1,128)S(1)}, u32[]{:S(2)}, u32[]{:S(2)}) async-start(f32[64,1,416]{2,1,0:T(1,128)} %reshape.312), calls=%async_computation | async-start | bytes 262144 | tf_op jit(solution)/shard_map/all_to_all | solution.py:51
  331.1 60.2 %copy-start.24 = (pred[16384]{0:T(1024)(128)(4,1)S(1)}, pred[16384]{0:T(1024)(128)(4,1)}, u32[]{:S(2)}) copy-start(pred[16384]{0:T(1024)(128)(4,1)} %compare_and_fusion) | copy-start | bytes 49156
  430.7 27.0 %copy-start.20 = (f32[2,52,128]{2,0,1:T(2,128)S(1)}, f32[2,52,128]{2,0,1:T(2,128)}, u32[]{:S(2)}) copy-start(f32[2,52,128]{2,0,1:T(2,128)} %fusion.15) | copy-start | bytes 159748
  430.7 27.0 %copy-start.21 = (f32[2,52,128]{2,0,1:T(2,128)S(1)}, f32[2,52,128]{2,0,1:T(2,128)}, u32[]{:S(2)}) copy-start(f32[2,52,128]{2,0,1:T(2,128)} %fusion.17) | copy-start | bytes 159748
  430.7 26.9 %copy-start.22 = (f32[2,52,128]{2,0,1:T(2,128)S(1)}, f32[2,52,128]{2,0,1:T(2,128)}, u32[]{:S(2)}) copy-start(f32[2,52,128]{2,0,1:T(2,128)} %fusion.14) | copy-start | bytes 159748
  430.8 26.9 %copy-start.23 = (f32[2,52,128]{2,0,1:T(2,128)S(1)}, f32[2,52,128]{2,0,1:T(2,128)}, u32[]{:S(2)}) copy-start(f32[2,52,128]{2,0,1:T(2,128)} %fusion.16) | copy-start | bytes 159748
  447.5 48.3 %copy-start.7 = (f32[2,2,52,128]{3,2,1,0:T(8,128)S(1)}, f32[2,2,52,128]{3,2,1,0:T(8,128)}, u32[]{:S(2)}) copy-start(f32[2,2,52,128]{3,2,1,0:T(8,128)} %copy-done.6) | copy-start | bytes 319492
  447.5 48.4 %copy-start.10 = (f32[1,2,128,128]{3,2,1,0:T(8,128)S(1)}, f32[1,2,128,128]{3,2,1,0:T(8,128)}, u32[]{:S(2)}) copy-start(f32[1,2,128,128]{3,2,1,0:T(8,128)} %get-tuple-element.22) | copy-start | bytes 393220
  447.5 48.4 %copy-start.12 = (f32[1,2,128,128]{3,2,1,0:T(8,128)S(1)}, f32[1,2,128,128]{3,2,1,0:T(8,128)}, u32[]{:S(2)}) copy-start(f32[1,2,128,128]{3,2,1,0:T(8,128)} %get-tuple-element.25) | copy-start | bytes 393220
  447.5 48.4 %copy-start.27 = (f32[52,128]{1,0:T(8,128)S(1)}, f32[52,128]{1,0:T(8,128)}, u32[]{:S(2)}) copy-start(f32[52,128]{1,0:T(8,128)} %get-tuple-element.30) | copy-start | bytes 79876
  447.5 160.4 %copy-start.33 = (f32[2]{0:T(128)S(1)}, f32[2]{0:T(128)}, u32[]{:S(2)}) copy-start(f32[2]{0:T(128)} %copy-done.32) | copy-start | bytes 28
  447.5 160.4 %copy-start.14 = (f32[52,128]{1,0:T(8,128)S(1)}, f32[52,128]{1,0:T(8,128)}, u32[]{:S(2)}) copy-start(f32[52,128]{1,0:T(8,128)} %copy-done.13) | copy-start | bytes 79876
  447.5 160.4 %copy-start.17 = (f32[2,2,52,128]{3,1,2,0:T(2,128)S(1)}, f32[2,2,52,128]{3,1,2,0:T(2,128)}, u32[]{:S(2)}) copy-start(f32[2,2,52,128]{3,1,2,0:T(2,128)} %param.12) | copy-start | bytes 319492
  447.5 160.4 %copy-start.29 = (f32[2,2,52,128]{3,1,2,0:T(2,128)S(1)}, f32[2,2,52,128]{3,1,2,0:T(2,128)}, u32[]{:S(2)}) copy-start(f32[2,2,52,128]{3,1,2,0:T(2,128)} %param.11) | copy-start | bytes 319492
  447.5 25.0 %all-to-all-start.1 = ((f32[64,1,416]{2,1,0:T(1,128)}), f32[64,1,416]{2,1,0:T(1,128)S(1)}, u32[]{:S(2)}, u32[]{:S(2)}) async-start(f32[64,1,416]{2,1,0:T(1,128)} %reshape.314), calls=%async_computation.1 | async-start | bytes 262144 | tf_op jit(solution)/shard_map/all_to_all | solution.py:133
  457.5 346.0 %reduce-scatter.2.cloned.1.call-start = ((), (), s32[]{:S(2)}) async-start(), calls=%async_computation.4 | async-start | bytes 147456 | tf_op jit(solution)/shard_map/reduce_scatter | solution.py:155
  457.7 151.6 %copy-start.4 = (f32[1,2,128,128]{3,2,0,1:T(8,128)S(1)}, f32[1,2,128,128]{3,2,0,1:T(8,128)}, u32[]{:S(2)}) copy-start(f32[1,2,128,128]{3,2,0,1:T(8,128)} %copy-done.2) | copy-start | bytes 393220
  457.7 151.6 %copy-start.19 = (f32[2,2,52,128]{3,2,1,0:T(8,128)S(1)}, f32[2,2,52,128]{3,2,1,0:T(8,128)}, u32[]{:S(2)}) copy-start(f32[2,2,52,128]{3,2,1,0:T(8,128)} %get-tuple-element.28) | copy-start | bytes 319492
  635.7 60.0 %copy-start.25 = (pred[16384]{0:T(1024)(128)(4,1)S(1)}, pred[16384]{0:T(1024)(128)(4,1)}, u32[]{:S(2)}) copy-start(pred[16384]{0:T(1024)(128)(4,1)} %compare_and_fusion) | copy-start | bytes 49156
  695.7 107.9 %copy-start.1 = (f32[16]{0:T(128)S(1)}, f32[16]{0:T(128)}, u32[]{:S(2)}) copy-start(f32[16]{0:T(128)} %param.16) | copy-start | bytes 196
  (13 other events, 108.4 us)
Sparse Core Ops, SparseCore 0:
  718.8 84.7 reduce-scatter.1
where the time goes:
time: 815 us; the launch traced here: 810 us
  blocking collectives  414 us (51%)
  local copies, waits for them, and re-layouts  208 us (26%)
  waiting for transfers between devices  97.6 us (12%)
  other arithmetic  43.7 us (5%)
  starting transfers between devices  16.8 us (2%)
  matrix products  15.8 us (2%)
  between operations  14.7 us (2%)
    psum x1, blocking collectives, on_device(): new_norm = lax.psum(norm_local, 'pw')  123 us
    gather x2, local copies, waits for them, and re-layouts, to_grid(): placed = jnp.take(padded, inverse_map, axis=0)  120 us
    psum x1, blocking collectives, on_device(): weights = lax.psum(correlation(all_occupied, direction), 'pw')  116 us
    psum x1, blocking collectives, on_device(): curvature = lax.psum(curvature_local, 'pw')  111 us
    reduce_scatter x1, waiting for transfers between devices, on_device(): lax.psum_scatter(density_local, 'band', scatter_dimension=1, tiled=True)  82.8 us
    all_gather x1, blocking collectives, on_device(): lax.all_gather(occupied_bands, 'band', axis=1, tiled=True) * sphere  42.5 us
    unnamed x80, local copies, waits for them, and re-layouts  30.2 us
    select_n x2, other arithmetic, to_grid(): placed = jnp.take(padded, inverse_map, axis=0)  26.3 us
  transfers between devices with their start and end apart: 3, of which 2 were waited for; matrix products, arithmetic and copies ran while one was open for 3% of the time, Pallas kernels for 0%

commit v1 on v0

v1 whole, which is shorter than its diff:
```python
import math

import jax
import jax.numpy as jnp
import numpy as np
from jax import lax
from jax.sharding import PartitionSpec as P

mode = lax.Precision.HIGH


def rotation(out_index, in_index, grid_len, sign):
    angles = (np.outer(out_index, in_index) % grid_len) * (2.0 * math.pi / grid_len)
    cosine = np.cos(angles)
    sine = np.sin(angles) * sign
    table = np.stack([np.stack([cosine, -sine]), np.stack([sine, cosine])])
    return jnp.asarray(table.astype(np.float32))


def signed_index(values, grid_len):
    return jnp.where(values < grid_len // 2, values, values - grid_len)


def wave_squares(columns, grid_len):
    wave_x = signed_index(columns // grid_len, grid_len)
    wave_y = signed_index(columns % grid_len, grid_len)
    wave_z = signed_index(jnp.arange(grid_len, dtype=jnp.int32), grid_len)
    return (wave_x * wave_x + wave_y * wave_y)[:, None] + (wave_z * wave_z)[None, :]


def halves(values):
    high = lax.reduce_precision(values, 8, 7)
    return high.astype(jnp.bfloat16), (values - high).astype(jnp.bfloat16)


def on_device(
    occupied_bands,
    iterate,
    residual,
    old_direction,
    preconditioner,
    old_norm,
    eigenvalues,
    band_slot,
    potential,
    column_map,
):
    f32 = jnp.float32
    grid_len = potential.shape[1]
    planes = potential.shape[0]
    owners = grid_len // planes
    nb = iterate.shape[1]
    cols = iterate.shape[2]
    slots = band_slot.shape[0]
    groups = slots // nb
    total_pw = column_map.shape[0] * grid_len
    box = grid_len // 2
    wide = -(-(cols + 1) // 8) * 8
    while planes * 2 * nb * (wide - cols) < nb + 2 * slots * nb:
        wide += 8
    spare = wide - cols
    full = np.arange(grid_len)
    inner = np.arange(box) - box // 2
    z_forward = rotation(full, full, grid_len, 1.0)
    z_inverse = rotation(full, full, grid_len, -1.0)
    out_table = rotation(full, inner, grid_len, 1.0)
    in_table = rotation(inner, full, grid_len, -1.0)

    by_owner = column_map.reshape(owners, cols)
    wave_x = signed_index(by_owner // grid_len, grid_len) + box // 2
    wave_y = signed_index(by_owner % grid_len, grid_len) + box // 2
    inside = (wave_x >= 0) & (wave_x < box) & (wave_y >= 0) & (wave_y < box)
    cell = jnp.where(inside, wave_x * box + wave_y, -1)
    cell = jnp.pad(cell, ((0, 0), (0, spare)), constant_values=-1).reshape(-1)
    low_count = min(256, box * box)
    high_count = box * box // low_count
    low_hot = (
        jnp.where(cell < 0, -1, cell % low_count)[:, None]
        == jnp.arange(low_count, dtype=jnp.int32)[None, :]
    ).astype(jnp.bfloat16)
    high_hot = (
        jnp.where(cell < 0, -1, cell // low_count)[None, :]
        == jnp.arange(high_count, dtype=jnp.int32)[:, None]
    )

    my_columns = lax.dynamic_slice_in_dim(column_map, lax.axis_index("pw") * cols, cols)
    squares = wave_squares(my_columns, grid_len)
    kinetic = squares.astype(f32) * (4.0 / (grid_len * grid_len))
    sphere = (squares < grid_len // 4 * (grid_len // 4)).astype(f32)
    occupied = occupied_bands * sphere
    start_wave = iterate * sphere
    masked_residual = residual * sphere
    previous = old_direction * sphere
    weight = preconditioner * sphere
    owner_ids = lax.dynamic_slice_in_dim(band_slot, lax.axis_index("band") * nb, nb)
    band_energy = jnp.sum(
        jnp.where(
            owner_ids[:, None] == jnp.arange(slots, dtype=jnp.int32)[None, :],
            eigenvalues[None, :],
            0.0,
        ),
        axis=1,
    )
    smoothed = weight[None] * masked_residual
    norm_local = jnp.sum(smoothed * masked_residual, axis=(0, 2, 3))

    rows = 2 * nb * cols
    copies = jnp.broadcast_to(occupied.reshape(1, rows, grid_len), (groups, rows, grid_len))
    all_occupied = lax.all_to_all(copies, "band", split_axis=0, concat_axis=0, tiled=True)
    all_occupied = all_occupied.reshape(groups, 2, nb, cols, grid_len)

    stacked = jnp.stack([occupied, start_wave, smoothed, previous], axis=1)
    stacked = jnp.pad(stacked, ((0, 0), (0, 0), (0, 0), (0, spare), (0, 0)))
    mixed = jnp.einsum("rqzk,qfnck->zrfnc", z_forward, stacked, precision=mode)
    mixed = mixed.reshape(owners, planes * 2 * 4, nb * wide)
    lane = jnp.pad(norm_local[:, None], ((0, 0), (cols, spare - 1))).reshape(-1)
    first_row = (jnp.arange(planes * 2 * 4) == 0).astype(f32)
    mixed = mixed + (first_row[:, None] * lane[None, :])[None]
    arrived = lax.all_to_all(mixed, "pw", split_axis=0, concat_axis=0, tiled=True)
    norms = jnp.sum(arrived[:, 0, :], axis=0).reshape(nb, wide)[:, cols]
    new_norm = norms / total_pw
    beta_ratio = new_norm / old_norm

    direction = smoothed + beta_ratio[None, :, None, None] * previous

    arrived = arrived.reshape(owners, planes, 2, 4, nb, wide)
    arrived = arrived.transpose(3, 2, 1, 4, 0, 5).reshape(4, 2 * planes, nb, owners * wide)
    moved = arrived[2] + beta_ratio[None, :, None] * arrived[3]
    fields = jnp.concatenate([arrived[:2], moved[None]], axis=0)
    fields = fields.reshape(3 * 2 * planes * nb, 1, owners * wide)
    high_part, low_part = halves(fields)
    zero = jnp.zeros((), jnp.bfloat16)
    spread = jnp.stack(
        [
            jnp.where(high_hot[None], high_part, zero),
            jnp.where(high_hot[None], low_part, zero),
        ]
    )
    placed = jnp.einsum("hrgc,cl->hrgl", spread, low_hot, preferred_element_type=f32)
    placed = (placed[0] + placed[1]).reshape(3, 2, planes, nb, box, box)
    grid = jnp.einsum("fqpnab,rqyb->frpnay", placed, out_table, precision=mode)
    grid = jnp.einsum("fqpnay,rqxa->frpnxy", grid, out_table, precision=mode)

    occupied_grid = grid[0]
    start_grid = grid[1]
    direction_grid = grid[2]
    started = jnp.sum(occupied_grid * start_grid, axis=(0, 2))
    changed = jnp.sum(occupied_grid * direction_grid, axis=0)
    weighted = potential[None, :, None] * direction_grid
    volume = float(grid_len**3)
    curvature_local = jnp.sum(weighted * direction_grid, axis=(0, 1, 3, 4)) / volume + jnp.sum(
        (kinetic[None, None] - band_energy[None, :, None, None]) * direction * direction,
        axis=(0, 2, 3),
    )
    over_re = jnp.einsum("gqvck,qnck->gvn", all_occupied, direction, precision=mode)
    over_im = jnp.einsum(
        "gvck,nck->gvn", all_occupied[:, 0], direction[1], precision=mode
    ) - jnp.einsum("gvck,nck->gvn", all_occupied[:, 1], direction[0], precision=mode)

    folded = jnp.einsum("qpnxy,rqax->rpnay", weighted, in_table, precision=mode)
    folded = jnp.einsum("qpnay,rqby->rpnab", folded, in_table, precision=mode)
    folded = folded.reshape(2 * planes * nb, high_count, low_count)
    both = jnp.stack(halves(folded))
    picked = jnp.einsum("hrgl,cl->hrgc", both, low_hot, preferred_element_type=f32)
    picked = picked[0] + picked[1]
    picked = jnp.sum(jnp.where(high_hot[None], picked, 0.0), axis=1)
    picked = picked.reshape(2, planes, nb, owners, wide).transpose(3, 1, 0, 2, 4)
    sums = jnp.concatenate([over_re.reshape(-1), over_im.reshape(-1), curvature_local])
    room = planes * 2 * nb * spare
    sums = jnp.pad(sums, (0, room - sums.shape[0])).reshape(1, planes, 2, nb, spare)
    sums = jnp.broadcast_to(sums, (owners,) + sums.shape[1:])
    outgoing = jnp.concatenate([picked[..., :cols], sums], axis=4)
    outgoing = outgoing.reshape(owners, planes * 2, nb * wide)
    returned = lax.all_to_all(outgoing, "pw", split_axis=0, concat_axis=0, tiled=True)
    returned = returned.reshape(owners, planes, 2, nb, wide)
    totals = jnp.sum(returned[..., cols:], axis=0).reshape(-1)
    pairs = slots * nb
    weights_re = totals[:pairs].reshape(groups, nb, nb)
    weights_im = totals[pairs : 2 * pairs].reshape(groups, nb, nb)
    curvature = (
        totals[2 * pairs : 2 * pairs + nb]
        + jnp.sum(weights_re * weights_re + weights_im * weights_im, axis=(0, 1))
    ) / total_pw
    step_size = new_norm / curvature

    density_local = started + jnp.sum(step_size[None, :, None, None] * changed, axis=1)
    density_local = density_local * (4.0 / total_pw)
    strip = grid_len // groups
    density_local = density_local.reshape(planes, groups, strip, grid_len).transpose(1, 0, 2, 3)
    density_local = density_local.reshape(groups, planes * strip, grid_len)
    density = lax.all_to_all(density_local, "band", split_axis=0, concat_axis=0, tiled=True)
    density = jnp.sum(density, axis=0).reshape(planes, strip, grid_len)

    returned = returned.reshape(grid_len, 2, nb, wide)
    local_potential = (
        jnp.einsum("zqnc,rqkz->rnck", returned, z_inverse, precision=mode)[:, :, :cols] / volume
    )
    projected_re = jnp.einsum(
        "gvck,gvn->nck", all_occupied[:, 0], weights_re, precision=mode
    ) - jnp.einsum("gvck,gvn->nck", all_occupied[:, 1], weights_im, precision=mode)
    projected_im = jnp.einsum(
        "gvck,gvn->nck", all_occupied[:, 0], weights_im, precision=mode
    ) + jnp.einsum("gvck,gvn->nck", all_occupied[:, 1], weights_re, precision=mode)
    image = (
        local_potential * sphere
        + (kinetic[None, None] - band_energy[None, :, None, None]) * direction
        + jnp.stack([projected_re, projected_im])
    )
    new_iterate = start_wave + step_size[None, :, None, None] * direction
    new_residual = masked_residual - step_size[None, :, None, None] * image
    return (new_iterate, new_residual, direction, new_norm, density)


def solution(mesh):
    in_specs = (
        P(None, "band", "pw", None),
        P(None, "band", "pw", None),
        P(None, "band", "pw", None),
        P(None, "band", "pw", None),
        P("band", "pw", None),
        P("band"),
        P(),
        P(),
        P("pw", None, None),
        P(),
    )
    out_specs = (
        P(None, "band", "pw", None),
        P(None, "band", "pw", None),
        P(None, "band", "pw", None),
        P("band"),
        P("pw", "band", None),
    )
    return jax.shard_map(
        on_device, mesh=mesh, in_specs=in_specs, out_specs=out_specs, check_vma=False
    )
```

time: 815 us -> 132 us (0.16)
  blocking collectives: 414 us -> 0 us
  local copies, waits for them, and re-layouts: 208 us -> 13 us
  waiting for transfers between devices: 97.6 us -> 54.4 us
  other arithmetic: 43.7 us -> 9.49 us
  starting transfers between devices: 16.8 us -> 39.7 us
  between operations: 14.7 us -> 1.23 us
    psum x3 -> x0, blocking collectives: 350 us -> none  [the longest x1 123 us: on_device(): new_norm = lax.psum(norm_local, 'pw')]
    gather x3 -> x0, local copies, waits for them, and re-layouts: 129 us -> none  [the longest x2 120 us: to_grid(): placed = jnp.take(padded, inverse_map, axis=0)]
    reduce_scatter x1 -> x0, waiting for transfers between devices: 82.8 us -> none  [on_device(): lax.psum_scatter(density_local, 'band', scatter_dimension=1, tiled=True)]
    all_gather x1 -> x0, blocking collectives: 42.5 us -> none  [on_device(): lax.all_gather(occupied_bands, 'band', axis=1, tiled=True) * sphere]
    all_to_all x2 -> x4, waiting for transfers between devices: 14.8 us -> 54.4 us  [the longest x1 27.1 us: on_device(): lax.all_to_all(mixed, 'pw', split_axis=0, concat_axis=0, tiled=True)]
    select_n x4 -> x3, other arithmetic: 28.7 us -> 1.32 us  [the longest x1 0.64 us: on_device(): jnp.where(high_hot[None], high_part, zero)]
    unnamed x80 -> x37, local copies, waits for them, and re-layouts: 30.2 us -> 2.82 us
    all_to_all x2 -> x4, starting transfers between devices: 16.7 us -> 39.7 us  [the longest x1 14.1 us: on_device(): lax.all_to_all(mixed, 'pw', split_axis=0, concat_axis=0, tiled=True)]
  transfers between devices with their start and end apart: 3 -> 4, of which waited for: 2 -> 4; matrix products, arithmetic and copies ran while one was open for 3% -> 6% of each run, Pallas kernels for 0% -> 0%
where the time goes in v1:
time: 132 us; the launch traced here: 131 us
  waiting for transfers between devices  54.4 us (41%)
  starting transfers between devices  39.7 us (30%)
  matrix products  13.1 us (10%)
  local copies, waits for them, and re-layouts  13 us (10%)
  other arithmetic  9.49 us (7%)
    all_to_all x1, waiting for transfers between devices, on_device(): lax.all_to_all(mixed, 'pw', split_axis=0, concat_axis=0, tiled=True)  27.1 us
    all_to_all x1, waiting for transfers between devices, on_device(): lax.all_to_all(outgoing, 'pw', split_axis=0, concat_axis=0, tiled=True)  14.3 us
    all_to_all x1, starting transfers between devices, on_device(): lax.all_to_all(mixed, 'pw', split_axis=0, concat_axis=0, tiled=True)  14.1 us
    all_to_all x1, starting transfers between devices, on_device(): lax.all_to_all(copies, 'band', split_axis=0, concat_axis=0, tiled=True)  10.3 us
    all_to_all x1, waiting for transfers between devices, on_device(): lax.all_to_all(copies, 'band', split_axis=0, concat_axis=0, tiled=True)  9.88 us
    all_to_all x1, starting transfers between devices, on_device(): lax.all_to_all(outgoing, 'pw', split_axis=0, concat_axis=0, tiled=True)  8.41 us
    all_to_all x1, starting transfers between devices, on_device(): lax.all_to_all(density_local, 'band', split_axis=0, concat_axis=0, tiled=...  6.91 us
    all_to_all x1, waiting for transfers between devices, on_device(): lax.all_to_all(density_local, 'band', split_axis=0, concat_axis=0, tiled=...  3.15 us
  transfers between devices with their start and end apart: 4, of which 4 were waited for; matrix products, arithmetic and copies ran while one was open for 6% of the time, Pallas kernels for 0%

profile of v1, /device:TPU:1, one launch (start us, length us, event | category | flops | bytes accessed | tf_op | source)
XLA Modules:
  0.0 130.9 jit_solution(4781665276272221555)
XLA Ops:
  0.7 0.8 fusion.64
  1.6 0.8 broadcast_multiply_fusion
  2.4 1.2 fusion.34
  3.6 1.0 broadcast_in_dim.118
  4.6 10.3 %all-to-all-start.1 = ((f32[8,208,128]{2,1,0:T(8,128)}), f32[8,208,128]{2,1,0:T(8,128)S(1)}, u32[]{:S(2)}, u32[]{:S(2)}) async-start(f32[8,208,128]{2,1,0:T(8,128)} %broadcast_in_dim.118), calls=%async_computation.1 | async-start | bytes 1703936 | tf_op jit(solution)/shard_map/all_to_all | solution.py:109
  15.4 0.8 copy.159
  17.1 0.8 broadcast_add_fusion
  17.9 9.9 %all-to-all-done.1 = f32[8,208,128]{2,1,0:T(8,128)S(1)} async-done(((f32[8,208,128]{2,1,0:T(8,128)}), f32[8,208,128]{2,1,0:T(8,128)S(1)}, u32[]{:S(2)}, u32[]{:S(2)}) %all-to-all-start.1) | async-done | bytes 852000 | tf_op jit(solution)/shard_map/all_to_all | solution.py:109
  27.8 14.1 %all-to-all-start = ((f32[64,16,128]{2,1,0:T(8,128)}), f32[64,16,128]{2,1,0:T(8,128)S(1)}, u32[]{:S(2)}, u32[]{:S(2)}) async-start(f32[64,16,128]{2,1,0:T(8,128)} %broadcast_add_fusion), calls=%async_computation | async-start | bytes 1048576 | tf_op jit(solution)/shard_map/all_to_all | solution.py:119
  44.2 27.1 %all-to-all-done = f32[64,16,128]{2,1,0:T(8,128)S(1)} async-done(((f32[64,16,128]{2,1,0:T(8,128)}), f32[64,16,128]{2,1,0:T(8,128)S(1)}, u32[]{:S(2)}, u32[]{:S(2)}) %all-to-all-start) | async-done | bytes 524320 | tf_op jit(solution)/shard_map/all_to_all | solution.py:119
  71.9 0.9 fusion.72
  73.4 1.0 copy.163
  76.6 1.9 %fusion = f32[2,24,16,256]{3,2,1,0:T(8,128)S(1)} fusion(bf16[1,24,16,4096]{3,2,1,0:T(8,128)(2,1)S(1)} %get-tuple-element.48, bf16[1,24,16,4096]{3,2,1,0:T(8,128)(2,1)S(1)} %get-tuple-element.47, s32[4096]{0:T(1024)S(1)} %copy-done.8), kind=kOutput, calls=%fused_computation | convolution fusion | flops 1614807040 | bytes 7094272 | tf_op jit(solution)/shard_map/hrgc,cl->hrgl/dot_general | solution.py:139
  79.3 0.8 convolution_bitcast_fusion
  81.3 1.0 fusion.5
  83.5 1.5 %convolution_bitcast_fusion.10 = f32[8,2,2]{0,2,1:T(2,128)S(1)} fusion(f32[8,2,2,52,128]{4,0,3,2,1:T(8,128)S(1)} %bitcast.205, f32[2,52,128]{2,1,0:T(8,128)S(1)} %get-tuple-element.46), kind=kOutput, calls=%fused_computation.25 | convolution fusion | flops 1277952 | bytes 483456 | tf_op jit(solution)/shard_map/gvck,nck->gvn/dot_general | solution.py:158
  85.0 1.5 %fusion.13 = f32[8,2,2]{0,2,1:T(2,128)S(1)} fusion(f32[8,2,2]{0,2,1:T(2,128)S(1)} %convolution_bitcast_fusion.10, f32[8,2,2,52,128]{4,0,3,2,1:T(8,128)S(1)} %bitcast.206, f32[2,52,128]{2,1,0:T(8,128)S(1)} %get-tuple-element.45), kind=kOutput, calls=%fused_computation.28 | convolution fusion | flops 1277984 | bytes 485504 | tf_op jit(solution)/shard_map/gvck,nck->gvn/dot_general | solution.py:156
  86.7 3.1 %convolution_bitcast_fusion.12 = f32[8,2,2]{0,2,1:T(2,128)S(1)} fusion(f32[8,2,2,52,128]{4,0,3,2,1:T(8,128)S(1)} %bitcast.207, f32[2,2,52,128,1]{3,2,0,1,4:T(8,128)S(1)} %bitcast.214), kind=kOutput, calls=%fused_computation.27 | convolution fusion | flops 2555904 | bytes 958592 | tf_op jit(solution)/shard_map/gqvck,qnck->gvn/dot_general | solution.py:155
  90.6 0.8 reshape.421
  91.5 8.4 %all-to-all-start.2 = ((f32[64,4,128]{2,1,0:T(4,128)}), f32[64,4,128]{2,1,0:T(4,128)S(1)}, u32[]{:S(2)}, u32[]{:S(2)}) async-start(f32[64,4,128]{2,1,0:T(4,128)} %reshape.421), calls=%async_computation.2 | async-start | bytes 262144 | tf_op jit(solution)/shard_map/all_to_all | solution.py:174
  99.9 0.7 copy.193
  100.6 14.3 %all-to-all-done.2 = f32[64,4,128]{2,1,0:T(4,128)S(1)} async-done(((f32[64,4,128]{2,1,0:T(4,128)}), f32[64,4,128]{2,1,0:T(4,128)S(1)}, u32[]{:S(2)}, u32[]{:S(2)}) %all-to-all-start.2) | async-done | bytes 131104 | tf_op jit(solution)/shard_map/all_to_all | solution.py:174
  118.1 6.9 %all-to-all-start.3 = ((f32[8,32,128]{2,1,0:T(8,128)}), f32[8,32,128]{2,1,0:T(8,128)S(1)}, u32[]{:S(2)}, u32[]{:S(2)}) async-start(f32[8,32,128]{2,1,0:T(8,128)} %bitcast.76), calls=%async_computation.3 | async-start | bytes 262144 | tf_op jit(solution)/shard_map/all_to_all | solution.py:191
  127.1 3.1 %all-to-all-done.3 = f32[8,32,128]{2,1,0:T(8,128)S(1)} async-done(((f32[8,32,128]{2,1,0:T(8,128)}), f32[8,32,128]{2,1,0:T(8,128)S(1)}, u32[]{:S(2)}, u32[]{:S(2)}) %all-to-all-start.3) | async-done | bytes 131104 | tf_op jit(solution)/shard_map/all_to_all | solution.py:191
  (118 shorter events, 16.8 us)
Async XLA Ops:
  0.6 14.3 %copy-start.14 = (f32[2,2,128,128,1,1]{3,2,1,0,5,4:T(8,128)S(1)}, f32[2,2,128,128,1,1]{3,2,1,0,5,4:T(8,128)}, u32[]{:S(2)}) copy-start(f32[2,2,128,128,1,1]{3,2,1,0,5,4:T(8,128)} %constant.155) | copy-start | bytes 786436
  4.6 23.2 %all-to-all-start.1 = ((f32[8,208,128]{2,1,0:T(8,128)}), f32[8,208,128]{2,1,0:T(8,128)S(1)}, u32[]{:S(2)}, u32[]{:S(2)}) async-start(f32[8,208,128]{2,1,0:T(8,128)} %broadcast_in_dim.118), calls=%async_computation.1 | async-start | bytes 1703936 | tf_op jit(solution)/shard_map/all_to_all | solution.py:109
  15.3 26.6 %copy-start.9 = (s32[3328]{0:T(1024)S(1)}, s32[3328]{0:T(1024)}, u32[]{:S(2)}) copy-start(s32[3328]{0:T(1024)} %param.23) | copy-start | bytes 39940
  15.3 26.8 %copy-start.6 = (f32[2,128,128]{2,1,0:T(8,128)S(1)}, f32[2,128,128]{2,1,0:T(8,128)}, u32[]{:S(2)}) copy-start(f32[2,128,128]{2,1,0:T(8,128)} %param.22) | copy-start | bytes 393220
  15.3 26.9 %copy-start.11 = (s32[16]{0:T(128)S(1)}, s32[16]{0:T(128)}, u32[]{:S(2)}) copy-start(s32[16]{0:T(128)} %param.21) | copy-start | bytes 196
  15.3 27.0 %copy-start.12 = (f32[16]{0:T(128)S(1)}, f32[16]{0:T(128)}, u32[]{:S(2)}) copy-start(f32[16]{0:T(128)} %param.20) | copy-start | bytes 196
  27.8 43.5 %all-to-all-start = ((f32[64,16,128]{2,1,0:T(8,128)}), f32[64,16,128]{2,1,0:T(8,128)S(1)}, u32[]{:S(2)}, u32[]{:S(2)}) async-start(f32[64,16,128]{2,1,0:T(8,128)} %broadcast_add_fusion), calls=%async_computation | async-start | bytes 1048576 | tf_op jit(solution)/shard_map/all_to_all | solution.py:119
  71.9 3.3 %copy-start.13 = (f32[2]{0:T(128)S(1)}, f32[2]{0:T(128)}, u32[]{:S(2)}) copy-start(f32[2]{0:T(128)} %param.19) | copy-start | bytes 28
  73.4 43.8 %copy-start.10 = (f32[2]{0:T(128)}, f32[2]{0:T(128)S(1)}, u32[]{:S(2)}) copy-start(f32[2]{0:T(128)S(1)} %multiply_reduce_fusion.2) | copy-start | bytes 28
  75.9 0.7 copy-start.8
  76.6 2.2 %copy-start.2 = (f32[2,2,128,64,1,1,1]{2,3,1,0,6,5,4:T(8,128)S(1)}, f32[2,2,128,64,1,1,1]{2,3,1,0,6,5,4:T(8,128)}, u32[]{:S(2)}) copy-start(f32[2,2,128,64,1,1,1]{2,3,1,0,6,5,4:T(8,128)} %constant.156) | copy-start | bytes 393220
  78.8 1.6 %copy-start.1 = (f32[2,2,64,128,1,1]{3,2,1,0,5,4:T(8,128)S(1)}, f32[2,2,64,128,1,1]{3,2,1,0,5,4:T(8,128)}, u32[]{:S(2)}) copy-start(f32[2,2,64,128,1,1]{3,2,1,0,5,4:T(8,128)} %constant.157) | copy-start | bytes 393220
  82.3 0.9 copy-start
  82.3 0.9 copy-start.4
  90.4 34.8 %copy-start.5 = (f32[2,2,128,128,1]{3,2,1,0,4:T(8,128)S(1)}, f32[2,2,128,128,1]{3,2,1,0,4:T(8,128)}, u32[]{:S(2)}) copy-start(f32[2,2,128,128,1]{3,2,1,0,4:T(8,128)} %constant.158) | copy-start | bytes 786436
  91.5 34.2 %copy-start.3 = (f32[2,2,52,128]{3,1,2,0:T(2,128)S(1)}, f32[2,2,52,128]{3,1,2,0:T(2,128)}, u32[]{:S(2)}) copy-start(f32[2,2,52,128]{3,1,2,0:T(2,128)} %param.15) | copy-start | bytes 319492
  91.5 34.2 %copy-start.7 = (f32[52,128]{1,0:T(8,128)S(1)}, f32[52,128]{1,0:T(8,128)}, u32[]{:S(2)}) copy-start(f32[52,128]{1,0:T(8,128)} %get-tuple-element.56) | copy-start | bytes 79876
  91.5 23.4 %all-to-all-start.2 = ((f32[64,4,128]{2,1,0:T(4,128)}), f32[64,4,128]{2,1,0:T(4,128)S(1)}, u32[]{:S(2)}, u32[]{:S(2)}) async-start(f32[64,4,128]{2,1,0:T(4,128)} %reshape.421), calls=%async_computation.2 | async-start | bytes 262144 | tf_op jit(solution)/shard_map/all_to_all | solution.py:174
  118.1 12.2 %all-to-all-start.3 = ((f32[8,32,128]{2,1,0:T(8,128)}), f32[8,32,128]{2,1,0:T(8,128)S(1)}, u32[]{:S(2)}, u32[]{:S(2)}) async-start(f32[8,32,128]{2,1,0:T(8,128)} %bitcast.76), calls=%async_computation.3 | async-start | bytes 262144 | tf_op jit(solution)/shard_map/all_to_all | solution.py:191

commit v2 on v1

--- a/solution.py
+++ b/solution.py
@@ -1,9 +1,12 @@
+import functools
 import math
 
 import jax
 import jax.numpy as jnp
 import numpy as np
 from jax import lax
+from jax.experimental import pallas as pl
+from jax.experimental.pallas import tpu as pltpu
 from jax.sharding import PartitionSpec as P
 
 mode = lax.Precision.HIGH
@@ -31,6 +34,83 @@
 def halves(values):
     high = lax.reduce_precision(values, 8, 7)
     return high.astype(jnp.bfloat16), (values - high).astype(jnp.bfloat16)
+
+
+def exchange_kernel(plan, *refs):
+    count = len(plan)
+    sources, targets = refs[:count], refs[count : 2 * count]
+    sems = refs[2 * count :]
+    barrier = pltpu.get_barrier_semaphore()
+    mesh_ids = pl.DeviceIdType.MESH
+    greeted = {}
+    for axis, size, _ in plan:
+        greeted[axis] = size
+    for axis, size in greeted.items():
+        me = lax.axis_index(axis)
+
+        @pl.loop(1, size)
+        def _(step, axis=axis, size=size, me=me):
+            pl.semaphore_signal(
+                barrier,
+                inc=1,
+                device_id={axis: lax.rem(me + step, size)},
+                device_id_type=mesh_ids,
+            )
+
+    pl.semaphore_wait(barrier, sum(size - 1 for size in greeted.values()))
+
+    def copy_of(which, step):
+        axis, size, whole = plan[which]
+        me = lax.axis_index(axis)
+        peer = lax.rem(me + step, size)
+        send_sem, recv_sem = sems[2 * which], sems[2 * which + 1]
+        return pltpu.make_async_remote_copy(
+            src_ref=sources[which] if whole else sources[which].at[peer],
+            dst_ref=targets[which].at[me],
+            send_sem=send_sem.at[step],
+            recv_sem=recv_sem.at[step],
+            device_id={axis: peer},
+            device_id_type=mesh_ids,
+        )
+
+    for which, (axis, size, whole) in enumerate(plan):
+        half = size // 2
+        copy_of(which, half).start()
+
+        @pl.loop(1, half)
+        def _(near, which=which, half=half, size=size):
+            copy_of(which, half - near).start()
+            copy_of(which, half + near).start()
+
+    for which, (axis, size, whole) in enumerate(plan):
+        me = lax.axis_index(axis)
+        if whole:
+            targets[which][me] = sources[which][...]
+        else:
+            targets[which][me] = sources[which][me]
+    for which, (axis, size, whole) in enumerate(plan):
+
+        @pl.loop(1, size)
+        def _(step, which=which):
+            copy_of(which, step).wait()
+
+
+def exchange(collective_id, plan, *arrays):
+    shapes, scratch = [], []
+    for (axis, size, whole), array in zip(plan, arrays):
+        shape = ((size,) + array.shape) if whole else array.shape
+        shapes.append(jax.ShapeDtypeStruct(shape, array.dtype))
+        scratch += [pltpu.SemaphoreType.DMA((size,)), pltpu.SemaphoreType.DMA((size,))]
+    return pl.pallas_call(
+        functools.partial(exchange_kernel, plan),
+        out_shape=shapes,
+        in_specs=[pl.BlockSpec(memory_space=pltpu.VMEM)] * len(arrays),
+        out_specs=[pl.BlockSpec(memory_space=pltpu.VMEM)] * len(arrays),
+        scratch_shapes=scratch,
+        compiler_params=pltpu.CompilerParams(
+            collective_id=collective_id, has_side_effects=True
+        ),
+    )(*arrays)
 
 
 def on_device(
@@ -104,11 +184,6 @@
     smoothed = weight[None] * masked_residual
     norm_local = jnp.sum(smoothed * masked_residual, axis=(0, 2, 3))
 
-    rows = 2 * nb * cols
-    copies = jnp.broadcast_to(occupied.reshape(1, rows, grid_len), (groups, rows, grid_len))
-    all_occupied = lax.all_to_all(copies, "band", split_axis=0, concat_axis=0, tiled=True)
-    all_occupied = all_occupied.reshape(groups, 2, nb, cols, grid_len)
-
     stacked = jnp.stack([occupied, start_wave, smoothed, previous], axis=1)
     stacked = jnp.pad(stacked, ((0, 0), (0, 0), (0, 0), (0, spare), (0, 0)))
     mixed = jnp.einsum("rqzk,qfnck->zrfnc", z_forward, stacked, precision=mode)
@@ -116,7 +191,13 @@
     lane = jnp.pad(norm_local[:, None], ((0, 0), (cols, spare - 1))).reshape(-1)
     first_row = (jnp.arange(planes * 2 * 4) == 0).astype(f32)
     mixed = mixed + (first_row[:, None] * lane[None, :])[None]
-    arrived = lax.all_to_all(mixed, "pw", split_axis=0, concat_axis=0, tiled=True)
+    arrived, all_occupied = exchange(
+        0,
+        (("pw", owners, False), ("band", groups, True)),
+        mixed,
+        occupied.reshape(2 * nb, cols, grid_len),
+    )
+    all_occupied = all_occupied.reshape(groups, 2, nb, cols, grid_len)
     norms = jnp.sum(arrived[:, 0, :], axis=0).reshape(nb, wide)[:, cols]
     new_norm = norms / total_pw
     beta_ratio = new_norm / old_norm
@@ -152,10 +233,9 @@
         (kinetic[None, None] - band_energy[None, :, None, None]) * direction * direction,
         axis=(0, 2, 3),
     )
-    over_re = jnp.einsum("gqvck,qnck->gvn", all_occupied, direction, precision=mode)
-    over_im = jnp.einsum(
-        "gvck,nck->gvn", all_occupied[:, 0], direction[1], precision=mode
-    ) - jnp.einsum("gvck,nck->gvn", all_occupied[:, 1], direction[0], precision=mode)
+    over = jnp.einsum("gqvck,rnck->qrgvn", all_occupied, direction, precision=mode)
+    over_re = over[0, 0] + over[1, 1]
+    over_im = over[0, 1] - over[1, 0]
 
     folded = jnp.einsum("qpnxy,rqax->rpnay", weighted, in_table, precision=mode)
     folded = jnp.einsum("qpnay,rqby->rpnab", folded, in_table, precision=mode)
@@ -171,7 +251,7 @@
     sums = jnp.broadcast_to(sums, (owners,) + sums.shape[1:])
     outgoing = jnp.concatenate([picked[..., :cols], sums], axis=4)
     outgoing = outgoing.reshape(owners, planes * 2, nb * wide)
-    returned = lax.all_to_all(outgoing, "pw", split_axis=0, concat_axis=0, tiled=True)
+    (returned,) = exchange(1, (("pw", owners, False),), outgoing)
     returned = returned.reshape(owners, planes, 2, nb, wide)
     totals = jnp.sum(returned[..., cols:], axis=0).reshape(-1)
     pairs = slots * nb
@@ -188,23 +268,21 @@
     strip = grid_len // groups
     density_local = density_local.reshape(planes, groups, strip, grid_len).transpose(1, 0, 2, 3)
     density_local = density_local.reshape(groups, planes * strip, grid_len)
-    density = lax.all_to_all(density_local, "band", split_axis=0, concat_axis=0, tiled=True)
+    (density,) = exchange(2, (("band", groups, False),), density_local)
     density = jnp.sum(density, axis=0).reshape(planes, strip, grid_len)
 
     returned = returned.reshape(grid_len, 2, nb, wide)
     local_potential = (
         jnp.einsum("zqnc,rqkz->rnck", returned, z_inverse, precision=mode)[:, :, :cols] / volume
     )
-    projected_re = jnp.einsum(
-        "gvck,gvn->nck", all_occupied[:, 0], weights_re, precision=mode
-    ) - jnp.einsum("gvck,gvn->nck", all_occupied[:, 1], weights_im, precision=mode)
-    projected_im = jnp.einsum(
-        "gvck,gvn->nck", all_occupied[:, 0], weights_im, precision=mode
-    ) + jnp.einsum("gvck,gvn->nck", all_occupied[:, 1], weights_re, precision=mode)
+    mixing = jnp.stack(
+        [jnp.stack([weights_re, weights_im]), jnp.stack([-weights_im, weights_re])]
+    )
+    projected = jnp.einsum("gqvck,qrgvn->rnck", all_occupied, mixing, precision=mode)
     image = (
         local_potential * sphere
         + (kinetic[None, None] - band_energy[None, :, None, None]) * direction
-        + jnp.stack([projected_re, projected_im])
+        + projected
     )
     new_iterate = start_wave + step_size[None, :, None, None] * direction
     new_residual = masked_residual - step_size[None, :, None, None] * image

time: 132 us -> 113 us (0.86)
  Pallas kernels: 0 us -> 76.5 us
  waiting for transfers between devices: 54.4 us -> 0 us
  starting transfers between devices: 39.7 us -> 0 us
  matrix products: 13.1 us -> 10.9 us
  other arithmetic: 9.49 us -> 11 us
    pallas_call x0 -> x3, Pallas kernels: none -> 76.5 us  [exchange(): pl.pallas_call(functools.partial(exchange_kernel, plan), out_shape=shapes...]
    all_to_all x4 -> x0, waiting for transfers between devices: 54.4 us -> none  [the longest x1 27.1 us: on_device(): lax.all_to_all(mixed, 'pw', split_axis=0, concat_axis=0, tiled=True)]
    all_to_all x4 -> x0, starting transfers between devices: 39.7 us -> none  [the longest x1 14.1 us: on_device(): lax.all_to_all(mixed, 'pw', split_axis=0, concat_axis=0, tiled=True)]
    dot_general x7 -> x2, matrix products: 7.3 us -> 4.08 us  [the longest x1 3.09 us: on_device(): jnp.einsum('gqvck,rnck->qrgvn', all_occupied, direction, precision=mode)]
    slice x3 -> x1, local copies, waits for them, and re-layouts: 1.93 us -> 0.04 us  [on_device(): moved = arrived[2] + beta_ratio[None, :, None] * arrived[3]]
    reshape x1 -> x2, local copies, waits for them, and re-layouts: 0.61 us -> 2.26 us  [on_device(): arrived = arrived.reshape(owners, planes, 2, 4, nb, wide)]
    unnamed x37 -> x35, local copies, waits for them, and re-layouts: 2.82 us -> 2.73 us
  transfers between devices with their start and end apart: 4 -> 0, of which waited for: 4 -> 0; matrix products, arithmetic and copies ran while one was open for 6% -> 0% of each run, Pallas kernels for 0% -> 0%
where the time goes in v2:
time: 113 us
  Pallas kernels  76.5 us (68%)
  local copies, waits for them, and re-layouts  13 us (12%)
  other arithmetic  11 us (10%)
  matrix products  10.9 us (10%)
  between operations  1.19 us (1%)
    pallas_call x3, Pallas kernels, exchange(): pl.pallas_call(functools.partial(exchange_kernel, plan), out_shape=shapes...  76.5 us
    dot_general x1, matrix products, on_device(): jnp.einsum('gqvck,rnck->qrgvn', all_occupied, direction, precision=mode)  3.09 us
    unnamed x35, local copies, waits for them, and re-layouts  2.73 us
    reshape x2, local copies, waits for them, and re-layouts, on_device(): arrived = arrived.reshape(owners, planes, 2, 4, nb, wide)  2.26 us

profile of v2, /device:TPU:1, one launch (start us, length us, event | category | flops | bytes accessed | tf_op | source)
XLA Modules:
  0.0 112.5 jit_solution(14532815576645956174)
XLA Ops:
  0.6 0.8 fusion.59
  1.5 0.8 broadcast_multiply_fusion
  2.4 1.2 %fusion.37 = (f32[2]{0:T(128)S(1)}, f32[2,1,2,52,128]{4,3,0,2,1:T(8,128)S(1)}, f32[2,2,52,128]{3,2,0,1:T(8,128)S(1)}, f32[2,1,2,52,128]{4,3,0,2,1:T(8,128)S(1)}, f32[2,1,2,52,128]{4,3,0,2,1:T(8,128)S(1)}) fusion(f32[2,2,52,128]{3,1,2,0:T(2,128)} %param.16, f32[2,52,128]{2,1,0:T(8,128)S(1)} %copy.140, f32[52,128]{1,0:T(8,128)S(1)} %fusion.49, ...), kind=kLoop, calls=%fused_computation.75 | loop fusion | flops 186366 | bytes 931848 | tf_op jit(solution)/shard_map/reduce_sum | solution.py:185
  3.6 1.4 %convolution_bitcast_fusion.2 = f32[128,2,4,2,64]{0,4,1,3,2:T(8,128)S(1)} fusion(f32[2,2,128,128,1,1]{3,2,1,0,5,4:T(8,128)} %constant.155, f32[2,1,2,52,128]{4,3,0,2,1:T(8,128)S(1)} %get-tuple-element.52, f32[2,1,2,52,128]{4,3,0,2,1:T(8,128)S(1)} %get-tuple-element.44, f32[2,1,2,52,128]{4,3,0,2,1:T(8,128)S(1)} %get-tuple-element.53, ...), kind=kOutput, calls=%fused_computation.17 | convolution fusion | flops 202375168 | bytes 1212416 | tf_op jit(solution)/shard_map/rqzk,qfnck->zrfnc/dot_general | solution.py:189
  4.9 0.8 copy.143
  6.7 0.8 broadcast_add_fusion.refs_0_
  7.5 0.7 copy.145
  8.2 46.3 %shard_map.173 = (f32[64,16,128]{2,1,0:T(8,128)}, f32[8,4,52,128]{3,2,1,0:T(8,128)}) custom-call(f32[64,16,128]{2,1,0:T(8,128)} %broadcast_add_fusion.refs_0_, f32[4,52,128]{2,1,0:T(8,128)} %bitcast.173), custom_call_target="tpu_custom_call" | custom-call | tf_op jit(solution)/shard_map/pallas_call | solution.py:104
  54.5 1.7 %reshape.388 = f32[64,2,2,4,2,64]{5,4,3,2,1,0:T(2,128)S(1)} reshape(f32[64,16,128]{2,1,0:T(8,128)} %get-tuple-element.7) | data formatting | bytes 1048576 | tf_op jit(solution)/shard_map/reshape | solution.py:207
  57.1 1.0 slice_reduce_fusion.1
  60.4 1.9 %fusion = f32[2,24,16,256]{3,2,1,0:T(8,128)S(1)} fusion(bf16[1,24,16,4096]{3,2,1,0:T(8,128)(2,1)S(1)} %get-tuple-element.50, bf16[1,24,16,4096]{3,2,1,0:T(8,128)(2,1)S(1)} %get-tuple-element.49, s32[4096]{0:T(1024)S(1)} %get-tuple-element.56), kind=kOutput, calls=%fused_computation | convolution fusion | flops 1614807040 | bytes 7094272 | tf_op jit(solution)/shard_map/hrgc,cl->hrgl/dot_general | solution.py:220
  63.2 0.8 convolution_bitcast_fusion
  65.0 1.0 fusion.5
  67.5 1.1 fusion.38
  68.6 3.1 %convolution_bitcast_fusion.7 = f32[2,2,8,2,2]{2,4,3,0,1:T(2,128)S(1)} fusion(f32[8,2,2,52,128]{4,3,2,1,0:T(8,128)S(1)} %bitcast.165, f32[2,2,52,128,1,1]{3,2,0,1,5,4:T(8,128)S(1)} %bitcast.167), kind=kOutput, calls=%fused_computation.22 | convolution fusion | flops 5111808 | bytes 958976 | tf_op jit(solution)/shard_map/gqvck,rnck->qrgvn/dot_general | solution.py:236
  72.8 0.9 reshape.393.refs_0_
  73.7 18.5 %shard_map.174 = f32[64,4,128]{2,1,0:T(4,128)} custom-call(f32[64,4,128]{2,1,0:T(4,128)} %reshape.393.refs_0_), custom_call_target="tpu_custom_call" | custom-call | tf_op jit(solution)/shard_map/pallas_call | solution.py:104
  92.2 1.2 %reshape.394 = f32[64,2,2,2,64]{4,3,2,1,0:T(2,128)S(1)} reshape(f32[64,4,128]{2,1,0:T(4,128)} %shard_map.174) | data formatting | bytes 262144 | tf_op jit(solution)/shard_map/reshape | solution.py:255
  95.2 11.7 %shard_map.175 = f32[8,32,128]{2,1,0:T(8,128)} custom-call(f32[8,32,128]{2,1,0:T(8,128)} %bitcast.171), custom_call_target="tpu_custom_call" | custom-call | tf_op jit(solution)/shard_map/pallas_call | solution.py:104
  106.9 1.5 %reduce_sum.119 = f32[32,128]{1,0:T(8,128)} reduce(f32[8,32,128]{2,1,0:T(8,128)} %shard_map.175, f32[]{:T(128)} %constant.122.clone.1), dimensions={0}, to_apply=%region_11.12 | reduce | flops 28672 | bytes 147460 | tf_op jit(solution)/shard_map/reduce_sum | solution.py:272
  108.7 1.0 convolution_bitcast_fusion.6
  110.4 0.7 copy.168
  111.1 0.7 copy.169
  111.8 0.7 copy.170
  (106 shorter events, 11.1 us)
Async XLA Ops:
  2.4 1.2 %copy-start.5 = (f32[2,52,128]{2,1,0:T(8,128)}, f32[2,52,128]{2,1,0:T(8,128)S(1)}, u32[]{:S(2)}) copy-start(f32[2,52,128]{2,1,0:T(8,128)S(1)} %copy.140) | copy-start | bytes 159748
  8.2 50.3 %copy-start.11 = (f32[2]{0:T(128)S(1)}, f32[2]{0:T(128)}, u32[]{:S(2)}) copy-start(f32[2]{0:T(128)} %param.19) | copy-start | bytes 28
  56.7 2.7 %copy-start.9 = (s32[3328]{0:T(1024)S(1)}, s32[3328]{0:T(1024)}, u32[]{:S(2)}) copy-start(s32[3328]{0:T(1024)} %param.23) | copy-start | bytes 39940
  58.4 35.8 %copy-start.10 = (f32[2]{0:T(128)}, f32[2]{0:T(128)S(1)}, u32[]{:S(2)}) copy-start(f32[2]{0:T(128)S(1)} %multiply_reduce_fusion.2) | copy-start | bytes 28
  60.4 2.2 %copy-start.4 = (f32[2,2,128,64,1,1,1]{2,3,1,0,6,5,4:T(8,128)S(1)}, f32[2,2,128,64,1,1,1]{2,3,1,0,6,5,4:T(8,128)}, u32[]{:S(2)}) copy-start(f32[2,2,128,64,1,1,1]{2,3,1,0,6,5,4:T(8,128)} %constant.156) | copy-start | bytes 393220
  62.4 1.6 %copy-start.8 = (f32[2,128,128]{2,1,0:T(8,128)S(1)}, f32[2,128,128]{2,1,0:T(8,128)}, u32[]{:S(2)}) copy-start(f32[2,128,128]{2,1,0:T(8,128)} %param.22) | copy-start | bytes 393220
  62.4 1.7 %copy-start.3 = (f32[2,2,64,128,1,1]{3,2,1,0,5,4:T(8,128)S(1)}, f32[2,2,64,128,1,1]{3,2,1,0,5,4:T(8,128)}, u32[]{:S(2)}) copy-start(f32[2,2,64,128,1,1]{3,2,1,0,5,4:T(8,128)} %constant.157) | copy-start | bytes 393220
  66.1 1.1 copy-start.12
  66.1 1.2 %copy-start.13 = (f32[16]{0:T(128)S(1)}, f32[16]{0:T(128)}, u32[]{:S(2)}) copy-start(f32[16]{0:T(128)} %param.20) | copy-start | bytes 196
  66.1 1.4 %copy-start.2 = (f32[2,2,52,128]{3,1,2,0:T(2,128)S(1)}, f32[2,2,52,128]{3,1,2,0:T(2,128)}, u32[]{:S(2)}) copy-start(f32[2,2,52,128]{3,1,2,0:T(2,128)} %param.16) | copy-start | bytes 319492
  66.1 2.5 %copy-start = (f32[8,4,52,128]{3,2,1,0:T(8,128)S(1)}, f32[8,4,52,128]{3,2,1,0:T(8,128)}, u32[]{:S(2)}) copy-start(f32[8,4,52,128]{3,2,1,0:T(8,128)} %get-tuple-element.8) | copy-start | bytes 2555908
  71.7 38.2 %copy-start.7 = (f32[2,2,128,128,1]{3,2,1,0,4:T(8,128)S(1)}, f32[2,2,128,128,1]{3,2,1,0,4:T(8,128)}, u32[]{:S(2)}) copy-start(f32[2,2,128,128,1]{3,2,1,0,4:T(8,128)} %constant.158) | copy-start | bytes 786436
  72.3 38.0 %copy-start.6 = (f32[2,2,52,128]{3,1,2,0:T(2,128)S(1)}, f32[2,2,52,128]{3,1,2,0:T(2,128)}, u32[]{:S(2)}) copy-start(f32[2,2,52,128]{3,1,2,0:T(2,128)} %param.15) | copy-start | bytes 319492
  92.2 17.5 %copy-start.1 = (f32[64,4,128]{2,1,0:T(4,128)S(1)}, f32[64,4,128]{2,1,0:T(4,128)}, u32[]{:S(2)}) copy-start(f32[64,4,128]{2,1,0:T(4,128)} %shard_map.174) | copy-start | bytes 393220

commit v3 on v2

--- a/solution.py
+++ b/solution.py
@@ -111,6 +111,186 @@
             collective_id=collective_id, has_side_effects=True
         ),
     )(*arrays)
+
+
+def greet(axes):
+    barrier = pltpu.get_barrier_semaphore()
+    for axis, size in axes:
+        me = lax.axis_index(axis)
+
+        @pl.loop(1, size)
+        def _(step, axis=axis, size=size, me=me):
+            pl.semaphore_signal(
+                barrier,
+                inc=1,
+                device_id={axis: lax.rem(me + step, size)},
+                device_id_type=pl.DeviceIdType.MESH,
+            )
+
+    return barrier, sum(size - 1 for _, size in axes)
+
+
+def sender(axis, size, source, target, sems):
+    me = lax.axis_index(axis)
+
+    def copy_of(step):
+        peer = lax.rem(me + step, size)
+        return pltpu.make_async_remote_copy(
+            src_ref=source(peer),
+            dst_ref=target(me),
+            send_sem=sems[0].at[step],
+            recv_sem=sems[1].at[step],
+            device_id={axis: peer},
+            device_id_type=pl.DeviceIdType.MESH,
+        )
+
+    def start():
+        half = size // 2
+        copy_of(half).start()
+
+        @pl.loop(1, half)
+        def _(near):
+            copy_of(half - near).start()
+            copy_of(half + near).start()
+
+    def wait():
+        @pl.loop(1, size)
+        def _(step):
+            copy_of(step).wait()
+
+    return start, wait
+
+
+def finish_kernel(
+    sizes,
+    outgoing,
+    all_occupied,
+    direction,
+    curvature_row,
+    norm_row,
+    started,
+    changed,
+    returned,
+    total_row,
+    density,
+    rows,
+    sums,
+    all_sums,
+    local_density,
+    strips,
+    *sems,
+):
+    owners, groups, nb, total_pw = sizes
+    pairs = groups * 2 * nb * nb
+    me, my_group = lax.axis_index("pw"), lax.axis_index("band")
+    barrier, greetings = greet((("pw", owners), ("band", groups)))
+
+    rows[...] = jnp.zeros_like(rows)
+
+    @pl.loop(0, groups)
+    def _(group):
+        real, imag = [], []
+        for there in range(nb):
+            occ_re = all_occupied[group, there]
+            occ_im = all_occupied[group, nb + there]
+            for here in range(nb):
+                dir_re, dir_im = direction[here], direction[nb + here]
+                real.append(jnp.sum(occ_re * dir_re + occ_im * dir_im, axis=0, keepdims=True))
+                imag.append(jnp.sum(occ_re * dir_im - occ_im * dir_re, axis=0, keepdims=True))
+        height = 2 * nb * nb
+        start = pl.multiple_of(group * height, height)
+        rows[pl.ds(start, height), :] = jnp.concatenate(real + imag, axis=0)
+
+    lanes = lax.dot_general(
+        jnp.ones((8, rows.shape[1]), jnp.float32),
+        rows[...],
+        (((1,), (1,)), ((), ())),
+        precision=lax.Precision.HIGHEST,
+        preferred_element_type=jnp.float32,
+    )
+    sums[...] = lanes[0:1] + curvature_row[...]
+    all_sums[me] = sums[...]
+    returned[me] = outgoing[me]
+    pl.semaphore_wait(barrier, greetings)
+
+    sums_start, sums_wait = sender(
+        "pw", owners, lambda peer: sums, lambda mine: all_sums.at[mine], sems[0:2]
+    )
+    back_start, back_wait = sender(
+        "pw",
+        owners,
+        lambda peer: outgoing.at[peer],
+        lambda mine: returned.at[mine],
+        sems[2:4],
+    )
+    dens_start, dens_wait = sender(
+        "band",
+        groups,
+        lambda peer: local_density.at[peer],
+        lambda mine: strips.at[mine],
+        sems[4:6],
+    )
+    sums_start()
+    back_start()
+    sums_wait()
+    totals = jnp.sum(all_sums[...], axis=0)
+    total_row[...] = totals
+    lane = lax.broadcasted_iota(jnp.int32, totals.shape, 1)
+    steps = []
+    for band in range(nb):
+        squares = jnp.where((lane < pairs) & (lax.rem(lane, nb) == band), totals * totals, 0.0)
+        own = jnp.where(lane == pairs + band, totals, 0.0)
+        curvature = jnp.sum(squares + own, axis=1, keepdims=True) / total_pw
+        norm = jnp.sum(
+            jnp.where(lane == band, norm_row[...], 0.0), axis=1, keepdims=True
+        )
+        steps.append(norm / curvature)
+    planes, width = started.shape[0], started.shape[1] // groups
+    for group in range(groups):
+        for plane in range(planes):
+            part = slice(group * width, (group + 1) * width)
+            value = started[plane, part, :]
+            for band in range(nb):
+                value = value + steps[band] * changed[plane, band, part, :]
+            local_density[group, plane * width : (plane + 1) * width, :] = value * (
+                4.0 / total_pw
+            )
+    strips[my_group] = local_density[my_group]
+    dens_start()
+    dens_wait()
+    density[...] = jnp.sum(strips[...], axis=0)
+    back_wait()
+
+
+def finish(sizes, outgoing, all_occupied, direction, curvature_row, norm_row, started, changed):
+    owners, groups, nb, _ = sizes
+    planes, grid_len = started.shape[0], started.shape[1]
+    f32 = jnp.float32
+    height = planes * grid_len // groups
+    vmem = pl.BlockSpec(memory_space=pltpu.VMEM)
+    lanes = curvature_row.shape[1]
+    sems = []
+    for size in (owners, owners, groups):
+        sems += [pltpu.SemaphoreType.DMA((size,)), pltpu.SemaphoreType.DMA((size,))]
+    return pl.pallas_call(
+        functools.partial(finish_kernel, sizes),
+        out_shape=[
+            jax.ShapeDtypeStruct(outgoing.shape, f32),
+            jax.ShapeDtypeStruct((1, lanes), f32),
+            jax.ShapeDtypeStruct((height, started.shape[2]), f32),
+        ],
+        in_specs=[vmem] * 7,
+        out_specs=[vmem] * 3,
+        scratch_shapes=[
+            pltpu.VMEM((lanes, grid_len), f32),
+            pltpu.VMEM((1, lanes), f32),
+            pltpu.VMEM((owners, 1, lanes), f32),
+            pltpu.VMEM((groups, height, started.shape[2]), f32),
+            pltpu.VMEM((groups, height, started.shape[2]), f32),
+        ]
+        + sems,
+        compiler_params=pltpu.CompilerParams(collective_id=1, has_side_effects=True),
+    )(outgoing, all_occupied, direction, curvature_row, norm_row, started, changed)
 
 
 def on_device(
@@ -135,9 +315,7 @@
     groups = slots // nb
     total_pw = column_map.shape[0] * grid_len
     box = grid_len // 2
-    wide = -(-(cols + 1) // 8) * 8
-    while planes * 2 * nb * (wide - cols) < nb + 2 * slots * nb:
-        wide += 8
+    wide = -(-(cols + 1) // 64) * 64
     spare = wide - cols
     full = np.arange(grid_len)
     inner = np.arange(box) - box // 2
@@ -197,7 +375,6 @@
         mixed,
         occupied.reshape(2 * nb, cols, grid_len),
     )
-    all_occupied = all_occupied.reshape(groups, 2, nb, cols, grid_len)
     norms = jnp.sum(arrived[:, 0, :], axis=0).reshape(nb, wide)[:, cols]
     new_norm = norms / total_pw
     beta_ratio = new_norm / old_norm
@@ -233,9 +410,6 @@
         (kinetic[None, None] - band_energy[None, :, None, None]) * direction * direction,
         axis=(0, 2, 3),
     )
-    over = jnp.einsum("gqvck,rnck->qrgvn", all_occupied, direction, precision=mode)
-    over_re = over[0, 0] + over[1, 1]
-    over_im = over[0, 1] - over[1, 0]
 
     folded = jnp.einsum("qpnxy,rqax->rpnay", weighted, in_table, precision=mode)
     folded = jnp.einsum("qpnay,rqby->rpnab", folded, in_table, precision=mode)
@@ -245,40 +419,34 @@
     picked = picked[0] + picked[1]
     picked = jnp.sum(jnp.where(high_hot[None], picked, 0.0), axis=1)
     picked = picked.reshape(2, planes, nb, owners, wide).transpose(3, 1, 0, 2, 4)
-    sums = jnp.concatenate([over_re.reshape(-1), over_im.reshape(-1), curvature_local])
-    room = planes * 2 * nb * spare
-    sums = jnp.pad(sums, (0, room - sums.shape[0])).reshape(1, planes, 2, nb, spare)
-    sums = jnp.broadcast_to(sums, (owners,) + sums.shape[1:])
-    outgoing = jnp.concatenate([picked[..., :cols], sums], axis=4)
-    outgoing = outgoing.reshape(owners, planes * 2, nb * wide)
-    (returned,) = exchange(1, (("pw", owners, False),), outgoing)
-    returned = returned.reshape(owners, planes, 2, nb, wide)
-    totals = jnp.sum(returned[..., cols:], axis=0).reshape(-1)
+    outgoing = picked.reshape(owners, planes * 2, nb * wide)
     pairs = slots * nb
-    weights_re = totals[:pairs].reshape(groups, nb, nb)
-    weights_im = totals[pairs : 2 * pairs].reshape(groups, nb, nb)
+    lanes = 128
+    returned, totals, density = finish(
+        (owners, groups, nb, float(total_pw)),
+        outgoing,
+        all_occupied,
+        direction.reshape(2 * nb, cols, grid_len),
+        jnp.pad(curvature_local, (2 * pairs, lanes - 2 * pairs - nb)).reshape(1, lanes),
+        jnp.pad(new_norm, (0, lanes - nb)).reshape(1, lanes),
+        started,
+        changed,
+    )
+    density = density.reshape(planes, grid_len // groups, grid_len)
+    totals = totals.reshape(-1)
+    found = totals[: 2 * pairs].reshape(groups, 2, nb, nb)
     curvature = (
-        totals[2 * pairs : 2 * pairs + nb]
-        + jnp.sum(weights_re * weights_re + weights_im * weights_im, axis=(0, 1))
+        totals[2 * pairs : 2 * pairs + nb] + jnp.sum(found * found, axis=(0, 1, 2))
     ) / total_pw
     step_size = new_norm / curvature
-
-    density_local = started + jnp.sum(step_size[None, :, None, None] * changed, axis=1)
-    density_local = density_local * (4.0 / total_pw)
-    strip = grid_len // groups
-    density_local = density_local.reshape(planes, groups, strip, grid_len).transpose(1, 0, 2, 3)
-    density_local = density_local.reshape(groups, planes * strip, grid_len)
-    (density,) = exchange(2, (("band", groups, False),), density_local)
-    density = jnp.sum(density, axis=0).reshape(planes, strip, grid_len)
 
     returned = returned.reshape(grid_len, 2, nb, wide)
     local_potential = (
         jnp.einsum("zqnc,rqkz->rnck", returned, z_inverse, precision=mode)[:, :, :cols] / volume
     )
-    mixing = jnp.stack(
-        [jnp.stack([weights_re, weights_im]), jnp.stack([-weights_im, weights_re])]
-    )
-    projected = jnp.einsum("gqvck,qrgvn->rnck", all_occupied, mixing, precision=mode)
+    mixing = jnp.stack([found, jnp.stack([-found[:, 1], found[:, 0]], axis=1)], axis=1)
+    all_occupied = all_occupied.reshape(groups, 2, nb, cols, grid_len)
+    projected = jnp.einsum("gqvck,gqrvn->rnck", all_occupied, mixing, precision=mode)
     image = (
         local_potential * sphere
         + (kinetic[None, None] - band_energy[None, :, None, None]) * direction

time: 113 us -> 106 us (0.938)
  Pallas kernels: 76.5 us -> 73.1 us
  matrix products: 10.9 us -> 7.74 us
  other arithmetic: 11 us -> 8.45 us
  local copies, waits for them, and re-layouts: 13 us -> 15.2 us
    pallas_call x3 -> x1, Pallas kernels: 76.5 us -> 46.3 us  [exchange(): pl.pallas_call(functools.partial(exchange_kernel, plan), out_shape=shapes...]
    pallas_call x0 -> x1, Pallas kernels: none -> 26.8 us  [finish(): pl.pallas_call(functools.partial(finish_kernel, sizes), out_shape=[jax.Sh...]
    dot_general x2 -> x1, matrix products: 4.08 us -> 0.98 us  [on_device(): jnp.einsum('gqvck,gqrvn->rnck', all_occupied, mixing, precision=mode)]
    reduce_sum x3 -> x1, other arithmetic: 1.97 us -> 0.04 us  [on_device(): jnp.sum(found * found, axis=(0, 1, 2))]
    reduce_sum x0 -> x2, local copies, waits for them, and re-layouts: none -> 1.58 us  [the longest x1 0.83 us: on_device(): changed = jnp.sum(occupied_grid * direction_grid, axis=0)]
    reshape x3 -> x4, local copies, waits for them, and re-layouts: 2.1 us -> 2.65 us  [the longest x1 1.09 us: on_device(): returned = returned.reshape(grid_len, 2, nb, wide)]
where the time goes in v3:
time: 106 us
  Pallas kernels  73.1 us (69%)
  local copies, waits for them, and re-layouts  15.2 us (14%)
  other arithmetic  8.45 us (8%)
  matrix products  7.74 us (7%)
  between operations  1.12 us (1%)
    pallas_call x1, Pallas kernels, exchange(): pl.pallas_call(functools.partial(exchange_kernel, plan), out_shape=shapes...  46.3 us
    pallas_call x1, Pallas kernels, finish(): pl.pallas_call(functools.partial(finish_kernel, sizes), out_shape=[jax.Sh...  26.8 us
    unnamed x35, local copies, waits for them, and re-layouts  3.06 us
    reshape x2, local copies, waits for them, and re-layouts, on_device(): arrived = arrived.reshape(owners, planes, 2, 4, nb, wide)  2.26 us

profile of v3, /device:TPU:1, one launch (start us, length us, event | category | flops | bytes accessed | tf_op | source)
XLA Modules:
  0.0 105.6 jit_solution(4763665403840526703)
XLA Ops:
  0.6 0.8 fusion.56
  1.5 0.8 broadcast_multiply_fusion
  2.4 1.2 %fusion.35 = (f32[2]{0:T(128)S(1)}, f32[2,1,2,52,128]{4,3,0,2,1:T(8,128)S(1)}, f32[2,2,52,128]{3,2,0,1:T(8,128)S(1)}, f32[2,1,2,52,128]{4,3,0,2,1:T(8,128)S(1)}, f32[2,1,2,52,128]{4,3,0,2,1:T(8,128)S(1)}) fusion(f32[2,2,52,128]{3,1,2,0:T(2,128)} %param.16, f32[2,52,128]{2,1,0:T(8,128)S(1)} %copy.116, f32[52,128]{1,0:T(8,128)S(1)} %fusion.46, ...), kind=kLoop, calls=%fused_computation.68 | loop fusion | flops 186366 | bytes 931848 | tf_op jit(solution)/shard_map/reduce_sum | solution.py:363
  3.6 1.4 %convolution_bitcast_fusion.2 = f32[128,2,4,2,64]{0,4,1,3,2:T(8,128)S(1)} fusion(f32[2,2,128,128,1,1]{3,2,1,0,5,4:T(8,128)} %constant.155, f32[2,1,2,52,128]{4,3,0,2,1:T(8,128)S(1)} %get-tuple-element.58, f32[2,1,2,52,128]{4,3,0,2,1:T(8,128)S(1)} %get-tuple-element.50, f32[2,1,2,52,128]{4,3,0,2,1:T(8,128)S(1)} %get-tuple-element.59, ...), kind=kOutput, calls=%fused_computation.17 | convolution fusion | flops 202375168 | bytes 1212416 | tf_op jit(solution)/shard_map/rqzk,qfnck->zrfnc/dot_general | solution.py:367
  4.9 0.8 copy.119
  6.6 0.8 broadcast_add_fusion.refs_0_
  7.5 0.7 copy.121
  8.1 46.3 %shard_map.173 = (f32[64,16,128]{2,1,0:T(8,128)}, f32[8,4,52,128]{3,2,1,0:T(8,128)}) custom-call(f32[64,16,128]{2,1,0:T(8,128)} %broadcast_add_fusion.refs_0_, f32[4,52,128]{2,1,0:T(8,128)} %bitcast.164), custom_call_target="tpu_custom_call" | custom-call | tf_op jit(solution)/shard_map/pallas_call | solution.py:104
  54.4 1.7 %reshape.386 = f32[64,2,2,4,2,64]{5,4,3,2,1,0:T(2,128)S(1)} reshape(f32[64,16,128]{2,1,0:T(8,128)} %get-tuple-element.10) | data formatting | bytes 1048576 | tf_op jit(solution)/shard_map/reshape | solution.py:384
  57.1 1.0 slice_reduce_fusion
  60.4 1.9 %fusion = f32[2,24,16,256]{3,2,1,0:T(8,128)S(1)} fusion(bf16[1,24,16,4096]{3,2,1,0:T(8,128)(2,1)S(1)} %get-tuple-element.56, bf16[1,24,16,4096]{3,2,1,0:T(8,128)(2,1)S(1)} %get-tuple-element.55, s32[4096]{0:T(1024)S(1)} %get-tuple-element.63), kind=kOutput, calls=%fused_computation | convolution fusion | flops 1614807040 | bytes 7094272 | tf_op jit(solution)/shard_map/hrgc,cl->hrgl/dot_general | solution.py:397
  63.2 0.8 convolution_bitcast_fusion
  66.5 1.0 fusion.5
  68.5 0.9 reshape.390.outgoing
  69.3 0.8 copy.130.changed
  70.2 0.8 copy.129.started
  70.9 0.7 copy.128
  71.6 26.8 %shard_map.174 = (f32[64,4,128]{2,1,0:T(4,128)}, f32[1,128]{1,0:T(1,128)}, f32[32,128]{1,0:T(8,128)}) custom-call(f32[64,4,128]{2,1,0:T(4,128)} %reshape.390.outgoing, f32[8,4,52,128]{3,2,1,0:T(8,128)} %get-tuple-element.11.all_occupied, f32[4,52,128]{2,1,0:T(8,128)} %bitcast.165, f32[1,128]{1,0:T(1,128)} %get-tuple-element.69.curvature_row, ...), custom_call_target="tpu_custom_call" | custom-call | tf_op jit(solution)/shard_map/pallas_call | solution.py:275
  99.2 0.7 fusion.60
  100.3 1.0 convolution_bitcast_fusion.6
  101.3 1.1 %reshape.395 = f32[128,2,2,64]{3,2,1,0:T(2,128)S(1)} reshape(f32[64,4,128]{2,1,0:T(4,128)} %get-tuple-element.13) | data formatting | bytes 262144 | tf_op jit(solution)/shard_map/reshape | solution.py:443
  102.9 0.7 copy.138
  103.6 0.7 copy.139
  104.3 0.7 copy.140
  (90 shorter events, 10.5 us)
Async XLA Ops:
  8.1 50.3 %copy-start.11 = (f32[2]{0:T(128)S(1)}, f32[2]{0:T(128)}, u32[]{:S(2)}) copy-start(f32[2]{0:T(128)} %param.19) | copy-start | bytes 28
  56.7 2.7 %copy-start.8 = (s32[3328]{0:T(1024)S(1)}, s32[3328]{0:T(1024)}, u32[]{:S(2)}) copy-start(s32[3328]{0:T(1024)} %param.23) | copy-start | bytes 39940
  58.4 40.8 %copy-start.10 = (f32[2]{0:T(128)}, f32[2]{0:T(128)S(1)}, u32[]{:S(2)}) copy-start(f32[2]{0:T(128)S(1)} %multiply_reduce_fusion.2) | copy-start | bytes 28
  60.4 2.2 %copy-start.3 = (f32[2,2,128,64,1,1,1]{2,3,1,0,6,5,4:T(8,128)S(1)}, f32[2,2,128,64,1,1,1]{2,3,1,0,6,5,4:T(8,128)}, u32[]{:S(2)}) copy-start(f32[2,2,128,64,1,1,1]{2,3,1,0,6,5,4:T(8,128)} %constant.156) | copy-start | bytes 393220
  62.3 1.7 %copy-start.7 = (f32[2,128,128]{2,1,0:T(8,128)S(1)}, f32[2,128,128]{2,1,0:T(8,128)}, u32[]{:S(2)}) copy-start(f32[2,128,128]{2,1,0:T(8,128)} %param.22) | copy-start | bytes 393220
  62.6 1.9 %copy-start.12 = (s32[16]{0:T(128)S(1)}, s32[16]{0:T(128)}, u32[]{:S(2)}) copy-start(s32[16]{0:T(128)} %param.21) | copy-start | bytes 196
  62.6 1.9 %copy-start.13 = (f32[16]{0:T(128)S(1)}, f32[16]{0:T(128)}, u32[]{:S(2)}) copy-start(f32[16]{0:T(128)} %param.20) | copy-start | bytes 196
  62.6 2.2 %copy-start.1 = (f32[2,2,52,128]{3,1,2,0:T(2,128)S(1)}, f32[2,2,52,128]{3,1,2,0:T(2,128)}, u32[]{:S(2)}) copy-start(f32[2,2,52,128]{3,1,2,0:T(2,128)} %param.16) | copy-start | bytes 319492
  62.6 2.2 %copy-start.5 = (f32[2,2,52,128]{3,1,2,0:T(2,128)S(1)}, f32[2,2,52,128]{3,1,2,0:T(2,128)}, u32[]{:S(2)}) copy-start(f32[2,2,52,128]{3,1,2,0:T(2,128)} %param.17) | copy-start | bytes 319492
  63.2 2.4 %copy-start.2 = (f32[2,2,64,128,1,1]{3,2,1,0,5,4:T(8,128)S(1)}, f32[2,2,64,128,1,1]{3,2,1,0,5,4:T(8,128)}, u32[]{:S(2)}) copy-start(f32[2,2,64,128,1,1]{3,2,1,0,5,4:T(8,128)} %constant.157) | copy-start | bytes 393220
  67.5 32.8 %copy-start = (f32[8,4,52,128]{3,2,1,0:T(8,128)S(1)}, f32[8,4,52,128]{3,2,1,0:T(8,128)}, u32[]{:S(2)}) copy-start(f32[8,4,52,128]{3,2,1,0:T(8,128)} %get-tuple-element.11.all_occupied) | copy-start | bytes 2555908
  68.2 34.2 %copy-start.6 = (f32[2,2,128,128,1]{3,2,1,0,4:T(8,128)S(1)}, f32[2,2,128,128,1]{3,2,1,0,4:T(8,128)}, u32[]{:S(2)}) copy-start(f32[2,2,128,128,1]{3,2,1,0,4:T(8,128)} %constant.158) | copy-start | bytes 786436
  68.2 34.6 %copy-start.4 = (f32[2,2,52,128]{3,1,2,0:T(2,128)S(1)}, f32[2,2,52,128]{3,1,2,0:T(2,128)}, u32[]{:S(2)}) copy-start(f32[2,2,52,128]{3,1,2,0:T(2,128)} %param.15) | copy-start | bytes 319492
  98.3 6.6 %copy-start.9 = (f32[32,128]{1,0:T(8,128)S(1)}, f32[32,128]{1,0:T(8,128)}, u32[]{:S(2)}) copy-start(f32[32,128]{1,0:T(8,128)} %get-tuple-element.14) | copy-start | bytes 49156

commit v4 on v3

--- a/solution.py
+++ b/solution.py
@@ -34,83 +34,6 @@
 def halves(values):
     high = lax.reduce_precision(values, 8, 7)
     return high.astype(jnp.bfloat16), (values - high).astype(jnp.bfloat16)
-
-
-def exchange_kernel(plan, *refs):
-    count = len(plan)
-    sources, targets = refs[:count], refs[count : 2 * count]
-    sems = refs[2 * count :]
-    barrier = pltpu.get_barrier_semaphore()
-    mesh_ids = pl.DeviceIdType.MESH
-    greeted = {}
-    for axis, size, _ in plan:
-        greeted[axis] = size
-    for axis, size in greeted.items():
-        me = lax.axis_index(axis)
-
-        @pl.loop(1, size)
-        def _(step, axis=axis, size=size, me=me):
-            pl.semaphore_signal(
-                barrier,
-                inc=1,
-                device_id={axis: lax.rem(me + step, size)},
-                device_id_type=mesh_ids,
-            )
-
-    pl.semaphore_wait(barrier, sum(size - 1 for size in greeted.values()))
-
-    def copy_of(which, step):
-        axis, size, whole = plan[which]
-        me = lax.axis_index(axis)
-        peer = lax.rem(me + step, size)
-        send_sem, recv_sem = sems[2 * which], sems[2 * which + 1]
-        return pltpu.make_async_remote_copy(
-            src_ref=sources[which] if whole else sources[which].at[peer],
-            dst_ref=targets[which].at[me],
-            send_sem=send_sem.at[step],
-            recv_sem=recv_sem.at[step],
-            device_id={axis: peer},
-            device_id_type=mesh_ids,
-        )
-
-    for which, (axis, size, whole) in enumerate(plan):
-        half = size // 2
-        copy_of(which, half).start()
-
-        @pl.loop(1, half)
-        def _(near, which=which, half=half, size=size):
-            copy_of(which, half - near).start()
-            copy_of(which, half + near).start()
-
-    for which, (axis, size, whole) in enumerate(plan):
-        me = lax.axis_index(axis)
-        if whole:
-            targets[which][me] = sources[which][...]
-        else:
-            targets[which][me] = sources[which][me]
-    for which, (axis, size, whole) in enumerate(plan):
-
-        @pl.loop(1, size)
-        def _(step, which=which):
-            copy_of(which, step).wait()
-
-
-def exchange(collective_id, plan, *arrays):
-    shapes, scratch = [], []
-    for (axis, size, whole), array in zip(plan, arrays):
-        shape = ((size,) + array.shape) if whole else array.shape
-        shapes.append(jax.ShapeDtypeStruct(shape, array.dtype))
-        scratch += [pltpu.SemaphoreType.DMA((size,)), pltpu.SemaphoreType.DMA((size,))]
-    return pl.pallas_call(
-        functools.partial(exchange_kernel, plan),
-        out_shape=shapes,
-        in_specs=[pl.BlockSpec(memory_space=pltpu.VMEM)] * len(arrays),
-        out_specs=[pl.BlockSpec(memory_space=pltpu.VMEM)] * len(arrays),
-        scratch_shapes=scratch,
-        compiler_params=pltpu.CompilerParams(
-            collective_id=collective_id, has_side_effects=True
-        ),
-    )(*arrays)
 
 
 def greet(axes):
@@ -159,6 +82,122 @@
             copy_of(step).wait()
 
     return start, wait
+
+
+def band_value(row, lane, band):
+    return jnp.sum(jnp.where(lane == band, row, 0.0), axis=1, keepdims=True)
+
+
+def begin_kernel(
+    sizes,
+    stacked,
+    table,
+    norm_row,
+    old_row,
+    occupied,
+    both_here,
+    moved_here,
+    all_occupied,
+    total_row,
+    both,
+    moved,
+    smooth,
+    former,
+    all_norms,
+    *sems,
+):
+    owners, groups, nb, total_pw = sizes
+    me, my_group = lax.axis_index("pw"), lax.axis_index("band")
+    barrier, greetings = greet((("pw", owners), ("band", groups)))
+    parts = table.shape[1] // owners
+
+    def mixed(field):
+        return sum(
+            lax.dot_general(
+                table[part],
+                stacked[part, field],
+                (((1,), (1,)), ((), ())),
+                precision=lax.Precision.HIGHEST,
+                preferred_element_type=jnp.float32,
+            )
+            for part in range(2)
+        )
+
+    for field in range(2):
+        value = mixed(field)
+        for part in range(parts):
+            both[:, part * 2 + field, :] = value[part * owners : (part + 1) * owners]
+    smooth[...] = mixed(2)
+    former[...] = mixed(3)
+    all_norms[me] = norm_row[...]
+    both_here[me] = both[me]
+    all_occupied[my_group] = occupied[...]
+    pl.semaphore_wait(barrier, greetings)
+
+    norm_start, norm_wait = sender(
+        "pw", owners, lambda peer: norm_row, lambda mine: all_norms.at[mine], sems[0:2]
+    )
+    both_start, both_wait = sender(
+        "pw", owners, lambda peer: both.at[peer], lambda mine: both_here.at[mine], sems[2:4]
+    )
+    move_start, move_wait = sender(
+        "pw", owners, lambda peer: moved.at[peer], lambda mine: moved_here.at[mine], sems[4:6]
+    )
+    occ_start, occ_wait = sender(
+        "band", groups, lambda peer: occupied, lambda mine: all_occupied.at[mine], sems[6:8]
+    )
+    norm_start()
+    both_start()
+    occ_start()
+    norm_wait()
+    totals = jnp.sum(all_norms[...], axis=0)
+    total_row[...] = totals
+    lane = lax.broadcasted_iota(jnp.int32, totals.shape, 1)
+    wide = stacked.shape[2] // nb
+    ratio_row = jnp.zeros((1, stacked.shape[2]), jnp.float32)
+    place = lax.broadcasted_iota(jnp.int32, ratio_row.shape, 1)
+    for band in range(nb):
+        ratio = band_value(totals, lane, band) / total_pw / band_value(old_row[...], lane, band)
+        ratio_row = jnp.where(place // wide == band, ratio, ratio_row)
+    for part in range(parts):
+        rows = slice(part * owners, (part + 1) * owners)
+        moved[:, part, :] = smooth[rows, :] + ratio_row * former[rows, :]
+    moved_here[me] = moved[me]
+    move_start()
+    occ_wait()
+    both_wait()
+    move_wait()
+
+
+def begin(sizes, stacked, table, norm_row, old_row, occupied):
+    owners, groups, _, _ = sizes
+    f32 = jnp.float32
+    vmem = pl.BlockSpec(memory_space=pltpu.VMEM)
+    lanes, width = norm_row.shape[1], stacked.shape[2]
+    parts = table.shape[1] // owners
+    sems = []
+    for size in (owners, owners, owners, groups):
+        sems += [pltpu.SemaphoreType.DMA((size,)), pltpu.SemaphoreType.DMA((size,))]
+    return pl.pallas_call(
+        functools.partial(begin_kernel, sizes),
+        out_shape=[
+            jax.ShapeDtypeStruct((owners, 2 * parts, width), f32),
+            jax.ShapeDtypeStruct((owners, parts, width), f32),
+            jax.ShapeDtypeStruct((groups,) + occupied.shape, f32),
+            jax.ShapeDtypeStruct((1, lanes), f32),
+        ],
+        in_specs=[vmem] * 5,
+        out_specs=[vmem] * 4,
+        scratch_shapes=[
+            pltpu.VMEM((owners, 2 * parts, width), f32),
+            pltpu.VMEM((owners, parts, width), f32),
+            pltpu.VMEM((parts * owners, width), f32),
+            pltpu.VMEM((parts * owners, width), f32),
+            pltpu.VMEM((owners, 1, lanes), f32),
+        ]
+        + sems,
+        compiler_params=pltpu.CompilerParams(collective_id=0, has_side_effects=True),
+    )(stacked, table, norm_row, old_row, occupied)
 
 
 def finish_kernel(
@@ -241,9 +280,7 @@
         squares = jnp.where((lane < pairs) & (lax.rem(lane, nb) == band), totals * totals, 0.0)
         own = jnp.where(lane == pairs + band, totals, 0.0)
         curvature = jnp.sum(squares + own, axis=1, keepdims=True) / total_pw
-        norm = jnp.sum(
-            jnp.where(lane == band, norm_row[...], 0.0), axis=1, keepdims=True
-        )
+        norm = band_value(norm_row[...], lane, band)
         steps.append(norm / curvature)
     planes, width = started.shape[0], started.shape[1] // groups
     for group in range(groups):
@@ -315,7 +352,7 @@
     groups = slots // nb
     total_pw = column_map.shape[0] * grid_len
     box = grid_len // 2
-    wide = -(-(cols + 1) // 64) * 64
+    wide = -(-cols // 64) * 64
     spare = wide - cols
     full = np.arange(grid_len)
     inner = np.arange(box) - box // 2
@@ -364,27 +401,26 @@
 
     stacked = jnp.stack([occupied, start_wave, smoothed, previous], axis=1)
     stacked = jnp.pad(stacked, ((0, 0), (0, 0), (0, 0), (0, spare), (0, 0)))
-    mixed = jnp.einsum("rqzk,qfnck->zrfnc", z_forward, stacked, precision=mode)
-    mixed = mixed.reshape(owners, planes * 2 * 4, nb * wide)
-    lane = jnp.pad(norm_local[:, None], ((0, 0), (cols, spare - 1))).reshape(-1)
-    first_row = (jnp.arange(planes * 2 * 4) == 0).astype(f32)
-    mixed = mixed + (first_row[:, None] * lane[None, :])[None]
-    arrived, all_occupied = exchange(
-        0,
-        (("pw", owners, False), ("band", groups, True)),
-        mixed,
+    stacked = stacked.reshape(2, 4, nb * wide, grid_len)
+    table = z_forward.reshape(2, 2, owners, planes, grid_len).transpose(1, 3, 0, 2, 4)
+    lanes = 128
+    sizes = (owners, groups, nb, float(total_pw))
+    arrived, moved, all_occupied, norms = begin(
+        sizes,
+        stacked,
+        table.reshape(2, planes * 2 * owners, grid_len),
+        jnp.pad(norm_local, (0, lanes - nb)).reshape(1, lanes),
+        jnp.pad(old_norm, (0, lanes - nb)).reshape(1, lanes),
         occupied.reshape(2 * nb, cols, grid_len),
     )
-    norms = jnp.sum(arrived[:, 0, :], axis=0).reshape(nb, wide)[:, cols]
-    new_norm = norms / total_pw
+    new_norm = norms[0, :nb] / total_pw
     beta_ratio = new_norm / old_norm
 
     direction = smoothed + beta_ratio[None, :, None, None] * previous
 
-    arrived = arrived.reshape(owners, planes, 2, 4, nb, wide)
-    arrived = arrived.transpose(3, 2, 1, 4, 0, 5).reshape(4, 2 * planes, nb, owners * wide)
-    moved = arrived[2] + beta_ratio[None, :, None] * arrived[3]
-    fields = jnp.concatenate([arrived[:2], moved[None]], axis=0)
+    arrived = arrived.reshape(owners, planes, 2, 2, nb, wide).transpose(3, 2, 1, 4, 0, 5)
+    moved = moved.reshape(owners, planes, 2, nb, wide).transpose(2, 1, 3, 0, 4)
+    fields = jnp.concatenate([arrived, moved[None]], axis=0)
     fields = fields.reshape(3 * 2 * planes * nb, 1, owners * wide)
     high_part, low_part = halves(fields)
     zero = jnp.zeros((), jnp.bfloat16)
@@ -421,9 +457,8 @@
     picked = picked.reshape(2, planes, nb, owners, wide).transpose(3, 1, 0, 2, 4)
     outgoing = picked.reshape(owners, planes * 2, nb * wide)
     pairs = slots * nb
-    lanes = 128
     returned, totals, density = finish(
-        (owners, groups, nb, float(total_pw)),
+        sizes,
         outgoing,
         all_occupied,
         direction.reshape(2 * nb, cols, grid_len),

time: 106 us -> 101 us (0.953)
  other arithmetic: 8.45 us -> 6.11 us
  matrix products: 7.74 us -> 6.35 us
  Pallas kernels: 73.1 us -> 71.9 us
    pallas_call x1, Pallas kernels: 46.3 us -> 44.1 us  [begin(): pl.pallas_call(functools.partial(begin_kernel, sizes), out_shape=[jax.Sha...]
    dot_general x1 -> x0, matrix products: 1.36 us -> none  [on_device(): mixed = jnp.einsum('rqzk,qfnck->zrfnc', z_forward, stacked, precision=mode)]
    reshape x4 -> x6, local copies, waits for them, and re-layouts: 2.93 us -> 3.69 us  [the longest x2 1.45 us: on_device(): arrived.reshape(owners, planes, 2, 2, nb, wide).transpose(3, 2, 1, 4, 0, 5)]
    unnamed x35 -> x37, local copies, waits for them, and re-layouts: 3.06 us -> 3 us
where the time goes in v4:
time: 101 us
  Pallas kernels  71.9 us (71%)
  local copies, waits for them, and re-layouts  15.1 us (15%)
  matrix products  6.35 us (6%)
  other arithmetic  6.11 us (6%)
  between operations  1.12 us (1%)
    pallas_call x1, Pallas kernels, begin(): pl.pallas_call(functools.partial(begin_kernel, sizes), out_shape=[jax.Sha...  44.1 us
    pallas_call x1, Pallas kernels, finish(): pl.pallas_call(functools.partial(finish_kernel, sizes), out_shape=[jax.Sh...  27.8 us
    unnamed x37, local copies, waits for them, and re-layouts  3 us

profile of v4, /device:TPU:1, one launch (start us, length us, event | category | flops | bytes accessed | tf_op | source)
XLA Modules:
  0.0 100.6 jit_solution(17672127134536948883)
XLA Ops:
  0.6 0.8 fusion.47
  1.5 0.8 broadcast_multiply_fusion
  2.4 1.2 %fusion.26 = (f32[2]{0:T(128)S(1)}, f32[2,1,2,52,128]{4,3,0,2,1:T(8,128)S(1)}, f32[2,2,52,128]{3,2,0,1:T(8,128)S(1)}, f32[2,1,2,52,128]{4,3,0,2,1:T(8,128)S(1)}, f32[2,1,2,52,128]{4,3,0,2,1:T(8,128)S(1)}) fusion(f32[2,2,52,128]{3,1,2,0:T(2,128)} %param.16, f32[2,52,128]{2,1,0:T(8,128)S(1)} %copy.116, f32[52,128]{1,0:T(8,128)S(1)} %fusion.37, ...), kind=kLoop, calls=%fused_computation.55 | loop fusion | flops 186366 | bytes 931848 | tf_op jit(solution)/shard_map/reduce_sum | solution.py:400
  3.6 0.9 pad.22.clone
  4.5 0.7 copy.120
  5.7 44.1 %shard_map.173 = (f32[64,8,128]{2,1,0:T(8,128)}, f32[64,4,128]{2,1,0:T(4,128)}, f32[8,4,52,128]{3,2,1,0:T(8,128)}, f32[1,128]{1,0:T(1,128)}) custom-call(f32[2,4,128,128]{3,2,1,0:T(8,128)} %bitcast.154, f32[2,256,128]{2,1,0:T(8,128)} %constant.158.table, f32[1,128]{1,0:T(1,128)} %get-tuple-element.73.norm_row, f32[1,128]{1,0:T(1,128)} %get-tuple-element.72.old_row, ...), custom_call_target="tpu_custom_call" | custom-call | tf_op jit(solution)/shard_map/pallas_call | solution.py:181
  49.8 1.3 %reshape.338 = f32[64,2,2,2,2,64]{5,4,3,2,1,0:T(2,128)S(1)} reshape(f32[64,8,128]{2,1,0:T(8,128)} %get-tuple-element.13) | data formatting | bytes 524288 | tf_op jit(solution)/shard_map/reshape | solution.py:421
  51.3 1.1 %reshape.339 = f32[64,2,2,2,64]{4,3,2,1,0:T(2,128)S(1)} reshape(f32[64,4,128]{2,1,0:T(4,128)} %get-tuple-element.14) | data formatting | bytes 262144 | tf_op jit(solution)/shard_map/reshape | solution.py:422
  53.2 0.6 broadcast_select_fusion.1
  53.9 1.9 %fusion = f32[2,24,16,256]{3,2,1,0:T(8,128)S(1)} fusion(bf16[1,24,16,4096]{3,2,1,0:T(8,128)(2,1)S(1)} %get-tuple-element.60, bf16[1,24,16,4096]{3,2,1,0:T(8,128)(2,1)S(1)} %get-tuple-element.59, s32[4096]{0:T(1024)S(1)} %get-tuple-element.67), kind=kOutput, calls=%fused_computation | convolution fusion | flops 1614807040 | bytes 7094272 | tf_op jit(solution)/shard_map/hrgc,cl->hrgl/dot_general | solution.py:433
  56.6 0.8 convolution_bitcast_fusion
  58.4 1.0 %fusion.5 = f32[2,8,16,4096]{3,2,1,0:T(8,128)S(1)} fusion(s32[4096]{0:T(1024)S(1)} %get-tuple-element.67, bf16[1,8,16,256]{3,2,1,0:T(8,128)(2,1)S(1)} %get-tuple-element.58, bf16[1,8,16,256]{3,2,1,0:T(8,128)(2,1)S(1)} %get-tuple-element.57), kind=kOutput, calls=%fused_computation.6 | convolution fusion | flops 537985024 | bytes 4341760 | tf_op jit(solution)/shard_map/hrgl,cl->hrgc/dot_general | solution.py:454
  60.5 0.8 reshape.343.outgoing
  62.8 0.8 copy.130.changed
  63.7 0.7 copy.129.started
  64.4 0.6 copy.128
  65.6 27.8 %shard_map.174 = (f32[64,4,128]{2,1,0:T(4,128)}, f32[1,128]{1,0:T(1,128)}, f32[32,128]{1,0:T(8,128)}) custom-call(f32[64,4,128]{2,1,0:T(4,128)} %reshape.343.outgoing, f32[8,4,52,128]{3,2,1,0:T(8,128)} %get-tuple-element.15.all_occupied, f32[4,52,128]{2,1,0:T(8,128)} %bitcast.160, f32[1,128]{1,0:T(1,128)} %pad_bitcast_fusion.1.curvature_row, ...), custom_call_target="tpu_custom_call" | custom-call | tf_op jit(solution)/shard_map/pallas_call | solution.py:312
  93.4 0.7 slice_bitcast_fusion.4
  94.2 0.7 fusion.51
  95.3 1.0 convolution_bitcast_fusion.5
  96.3 1.1 %reshape.348 = f32[128,2,2,64]{3,2,1,0:T(2,128)S(1)} reshape(f32[64,4,128]{2,1,0:T(4,128)} %get-tuple-element.17) | data formatting | bytes 262144 | tf_op jit(solution)/shard_map/reshape | solution.py:478
  97.9 0.7 copy.138
  98.6 0.7 copy.139
  99.3 0.7 copy.140
  (81 shorter events, 7.9 us)
Async XLA Ops:
  0.6 4.5 %copy-start.10 = (f32[2]{0:T(128)S(1)}, f32[2]{0:T(128)}, u32[]{:S(2)}) copy-start(f32[2]{0:T(128)} %param.19) | copy-start | bytes 28
  49.8 3.1 %copy-start.8 = (s32[3328]{0:T(1024)S(1)}, s32[3328]{0:T(1024)}, u32[]{:S(2)}) copy-start(s32[3328]{0:T(1024)} %param.23) | copy-start | bytes 39940
  53.8 2.2 %copy-start.3 = (f32[2,2,128,64,1,1,1]{2,3,1,0,6,5,4:T(8,128)S(1)}, f32[2,2,128,64,1,1,1]{2,3,1,0,6,5,4:T(8,128)}, u32[]{:S(2)}) copy-start(f32[2,2,128,64,1,1,1]{2,3,1,0,6,5,4:T(8,128)} %constant.159) | copy-start | bytes 393220
  55.8 1.6 %copy-start.7 = (f32[2,128,128]{2,1,0:T(8,128)S(1)}, f32[2,128,128]{2,1,0:T(8,128)}, u32[]{:S(2)}) copy-start(f32[2,128,128]{2,1,0:T(8,128)} %param.22) | copy-start | bytes 393220
  55.8 1.7 %copy-start.2 = (f32[2,2,64,128,1,1]{3,2,1,0,5,4:T(8,128)S(1)}, f32[2,2,64,128,1,1]{3,2,1,0,5,4:T(8,128)}, u32[]{:S(2)}) copy-start(f32[2,2,64,128,1,1]{3,2,1,0,5,4:T(8,128)} %constant.160) | copy-start | bytes 393220
  59.5 2.1 %copy-start.12 = (f32[1,128]{1,0:T(1,128)S(1)}, f32[1,128]{1,0:T(1,128)}, u32[]{:S(2)}) copy-start(f32[1,128]{1,0:T(1,128)} %get-tuple-element.12) | copy-start | bytes 1540
  59.5 2.2 %copy-start.13 = (s32[16]{0:T(128)S(1)}, s32[16]{0:T(128)}, u32[]{:S(2)}) copy-start(s32[16]{0:T(128)} %param.21) | copy-start | bytes 196
  59.5 2.3 %copy-start.14 = (f32[16]{0:T(128)S(1)}, f32[16]{0:T(128)}, u32[]{:S(2)}) copy-start(f32[16]{0:T(128)} %param.20) | copy-start | bytes 196
  59.5 2.5 %copy-start.1 = (f32[2,2,52,128]{3,1,2,0:T(2,128)S(1)}, f32[2,2,52,128]{3,1,2,0:T(2,128)}, u32[]{:S(2)}) copy-start(f32[2,2,52,128]{3,1,2,0:T(2,128)} %param.16) | copy-start | bytes 319492
  59.5 2.5 %copy-start.5 = (f32[2,2,52,128]{3,1,2,0:T(2,128)S(1)}, f32[2,2,52,128]{3,1,2,0:T(2,128)}, u32[]{:S(2)}) copy-start(f32[2,2,52,128]{3,1,2,0:T(2,128)} %param.17) | copy-start | bytes 319492
  60.2 35.1 %copy-start = (f32[8,4,52,128]{3,2,1,0:T(8,128)S(1)}, f32[8,4,52,128]{3,2,1,0:T(8,128)}, u32[]{:S(2)}) copy-start(f32[8,4,52,128]{3,2,1,0:T(8,128)} %get-tuple-element.15.all_occupied) | copy-start | bytes 2555908
  61.5 35.9 %copy-start.6 = (f32[2,2,128,128,1]{3,2,1,0,4:T(8,128)S(1)}, f32[2,2,128,128,1]{3,2,1,0,4:T(8,128)}, u32[]{:S(2)}) copy-start(f32[2,2,128,128,1]{3,2,1,0,4:T(8,128)} %constant.161) | copy-start | bytes 786436
  61.5 36.3 %copy-start.4 = (f32[2,2,52,128]{3,1,2,0:T(2,128)S(1)}, f32[2,2,52,128]{3,1,2,0:T(2,128)}, u32[]{:S(2)}) copy-start(f32[2,2,52,128]{3,1,2,0:T(2,128)} %param.15) | copy-start | bytes 319492
  61.6 36.3 %copy-start.11 = (f32[2]{0:T(128)}, f32[2]{0:T(128)S(1)}, u32[]{:S(2)}) copy-start(f32[2]{0:T(128)S(1)} %get-tuple-element.82) | copy-start | bytes 28
  93.4 6.6 %copy-start.9 = (f32[32,128]{1,0:T(8,128)S(1)}, f32[32,128]{1,0:T(8,128)}, u32[]{:S(2)}) copy-start(f32[32,128]{1,0:T(8,128)} %get-tuple-element.18) | copy-start | bytes 49156

commit v5 on v4

--- a/solution.py
+++ b/solution.py
@@ -95,10 +95,11 @@
     norm_row,
     old_row,
     occupied,
+    fields,
+    all_occupied,
+    total_row,
     both_here,
     moved_here,
-    all_occupied,
-    total_row,
     both,
     moved,
     smooth,
@@ -126,7 +127,7 @@
     for field in range(2):
         value = mixed(field)
         for part in range(parts):
-            both[:, part * 2 + field, :] = value[part * owners : (part + 1) * owners]
+            both[:, field * parts + part, :] = value[part * owners : (part + 1) * owners]
     smooth[...] = mixed(2)
     former[...] = mixed(3)
     all_norms[me] = norm_row[...]
@@ -166,7 +167,20 @@
     move_start()
     occ_wait()
     both_wait()
+
+    def join(source, height):
+        @pl.loop(0, owners // 2)
+        def _(pair):
+            first, second = source[2 * pair], source[2 * pair + 1]
+            spot = pl.ds(pl.multiple_of(pair * 2 * wide, 2 * wide), 2 * wide)
+            near = lax.broadcasted_iota(jnp.int32, first.shape, 1) < wide
+            rows = slice(height, height + first.shape[0])
+            fields[0, rows, spot] = jnp.where(near, first, pltpu.roll(second, wide, 1))
+            fields[1, rows, spot] = jnp.where(near, pltpu.roll(first, wide, 1), second)
+
+    join(both_here, 0)
     move_wait()
+    join(moved_here, 2 * parts)
 
 
 def begin(sizes, stacked, table, norm_row, old_row, occupied):
@@ -181,14 +195,15 @@
     return pl.pallas_call(
         functools.partial(begin_kernel, sizes),
         out_shape=[
-            jax.ShapeDtypeStruct((owners, 2 * parts, width), f32),
-            jax.ShapeDtypeStruct((owners, parts, width), f32),
+            jax.ShapeDtypeStruct((2, 3 * parts, owners * width // 2), f32),
             jax.ShapeDtypeStruct((groups,) + occupied.shape, f32),
             jax.ShapeDtypeStruct((1, lanes), f32),
         ],
         in_specs=[vmem] * 5,
-        out_specs=[vmem] * 4,
+        out_specs=[vmem] * 3,
         scratch_shapes=[
+            pltpu.VMEM((owners, 2 * parts, width), f32),
+            pltpu.VMEM((owners, parts, width), f32),
             pltpu.VMEM((owners, 2 * parts, width), f32),
             pltpu.VMEM((owners, parts, width), f32),
             pltpu.VMEM((parts * owners, width), f32),
@@ -280,7 +295,7 @@
         squares = jnp.where((lane < pairs) & (lax.rem(lane, nb) == band), totals * totals, 0.0)
         own = jnp.where(lane == pairs + band, totals, 0.0)
         curvature = jnp.sum(squares + own, axis=1, keepdims=True) / total_pw
-        norm = band_value(norm_row[...], lane, band)
+        norm = band_value(norm_row[...], lane, band) / total_pw
         steps.append(norm / curvature)
     planes, width = started.shape[0], started.shape[1] // groups
     for group in range(groups):
@@ -401,11 +416,12 @@
 
     stacked = jnp.stack([occupied, start_wave, smoothed, previous], axis=1)
     stacked = jnp.pad(stacked, ((0, 0), (0, 0), (0, 0), (0, spare), (0, 0)))
+    assert nb == 2 and nb * wide == 128
     stacked = stacked.reshape(2, 4, nb * wide, grid_len)
     table = z_forward.reshape(2, 2, owners, planes, grid_len).transpose(1, 3, 0, 2, 4)
     lanes = 128
     sizes = (owners, groups, nb, float(total_pw))
-    arrived, moved, all_occupied, norms = begin(
+    fields, all_occupied, norms = begin(
         sizes,
         stacked,
         table.reshape(2, planes * 2 * owners, grid_len),
@@ -418,9 +434,6 @@
 
     direction = smoothed + beta_ratio[None, :, None, None] * previous
 
-    arrived = arrived.reshape(owners, planes, 2, 2, nb, wide).transpose(3, 2, 1, 4, 0, 5)
-    moved = moved.reshape(owners, planes, 2, nb, wide).transpose(2, 1, 3, 0, 4)
-    fields = jnp.concatenate([arrived, moved[None]], axis=0)
     fields = fields.reshape(3 * 2 * planes * nb, 1, owners * wide)
     high_part, low_part = halves(fields)
     zero = jnp.zeros((), jnp.bfloat16)
@@ -431,8 +444,8 @@
         ]
     )
     placed = jnp.einsum("hrgc,cl->hrgl", spread, low_hot, preferred_element_type=f32)
-    placed = (placed[0] + placed[1]).reshape(3, 2, planes, nb, box, box)
-    grid = jnp.einsum("fqpnab,rqyb->frpnay", placed, out_table, precision=mode)
+    placed = (placed[0] + placed[1]).reshape(nb, 3, planes, 2, box, box)
+    grid = jnp.einsum("nfpqab,rqyb->frpnay", placed, out_table, precision=mode)
     grid = jnp.einsum("fqpnay,rqxa->frpnxy", grid, out_table, precision=mode)
 
     occupied_grid = grid[0]
@@ -463,7 +476,7 @@
         all_occupied,
         direction.reshape(2 * nb, cols, grid_len),
         jnp.pad(curvature_local, (2 * pairs, lanes - 2 * pairs - nb)).reshape(1, lanes),
-        jnp.pad(new_norm, (0, lanes - nb)).reshape(1, lanes),
+        norms,
         started,
         changed,
     )

time: 101 us -> 101 us (level)
  Pallas kernels: 71.9 us -> 74.1 us
  local copies, waits for them, and re-layouts: 15.1 us -> 13 us
    reshape x5 -> x0, local copies, waits for them, and re-layouts: 3.1 us -> none  [the longest x2 1.45 us: on_device(): arrived.reshape(owners, planes, 2, 2, nb, wide).transpose(3, 2, 1, 4, 0, 5)]
    pallas_call x1, Pallas kernels: 44.1 us -> 46.4 us  [begin(): pl.pallas_call(functools.partial(begin_kernel, sizes), out_shape=[jax.Sha...]
    unnamed x37 -> x39, local copies, waits for them, and re-layouts: 3 us -> 3.1 us
where the time goes in v5:
time: 101 us
  Pallas kernels  74.1 us (73%)
  local copies, waits for them, and re-layouts  13 us (13%)
  matrix products  6.36 us (6%)
  other arithmetic  6.04 us (6%)
  between operations  1.09 us (1%)
    pallas_call x1, Pallas kernels, begin(): pl.pallas_call(functools.partial(begin_kernel, sizes), out_shape=[jax.Sha...  46.4 us
    pallas_call x1, Pallas kernels, finish(): pl.pallas_call(functools.partial(finish_kernel, sizes), out_shape=[jax.Sh...  27.8 us
    unnamed x39, local copies, waits for them, and re-layouts  3.1 us

profile of v5, /device:TPU:1, one launch (start us, length us, event | category | flops | bytes accessed | tf_op | source)
XLA Modules:
  0.0 100.6 jit_solution(1973954902393660379)
XLA Ops:
  0.6 0.8 fusion.47
  1.5 0.8 broadcast_multiply_fusion
  2.4 1.2 %fusion.26 = (f32[2]{0:T(128)S(1)}, f32[2,1,2,52,128]{4,3,0,2,1:T(8,128)S(1)}, f32[2,2,52,128]{3,2,0,1:T(8,128)S(1)}, f32[2,1,2,52,128]{4,3,0,2,1:T(8,128)S(1)}, f32[2,1,2,52,128]{4,3,0,2,1:T(8,128)S(1)}) fusion(f32[2,2,52,128]{3,1,2,0:T(2,128)} %param.16, f32[2,52,128]{2,1,0:T(8,128)S(1)} %copy.109, f32[52,128]{1,0:T(8,128)S(1)} %fusion.37, ...), kind=kLoop, calls=%fused_computation.52 | loop fusion | flops 186366 | bytes 931848 | tf_op jit(solution)/shard_map/reduce_sum | solution.py:415
  3.7 0.9 pad.19.clone
  4.5 0.7 copy.113
  5.7 46.4 %shard_map.173 = (f32[2,12,4096]{2,1,0:T(8,128)}, f32[8,4,52,128]{3,2,1,0:T(8,128)}, f32[1,128]{1,0:T(1,128)}) custom-call(f32[2,4,128,128]{3,2,1,0:T(8,128)} %bitcast.143, f32[2,256,128]{2,1,0:T(8,128)} %constant.156.table, f32[1,128]{1,0:T(1,128)} %get-tuple-element.71.norm_row, f32[1,128]{1,0:T(1,128)} %get-tuple-element.70.old_row, f32[4,52,128]{2,1,0:T(8,128)} %bitcast.147), custom_call_target="tpu_custom_call" | custom-call | tf_op jit(solution)/shard_map/pallas_call | solution.py:195
  52.1 1.1 %reshape.329 = f32[24,4096]{1,0:T(8,128)S(1)} reshape(f32[2,12,4096]{2,1,0:T(8,128)} %get-tuple-element.12) | data formatting | bytes 786432 | tf_op jit(solution)/shard_map/reshape | solution.py:437
  53.5 0.6 broadcast_select_fusion.1
  54.2 1.9 %fusion = f32[2,24,16,256]{3,2,1,0:T(8,128)S(1)} fusion(bf16[1,24,16,4096]{3,2,1,0:T(8,128)(2,1)S(1)} %get-tuple-element.58, bf16[1,24,16,4096]{3,2,1,0:T(8,128)(2,1)S(1)} %get-tuple-element.57, s32[4096]{0:T(1024)S(1)} %get-tuple-element.65), kind=kOutput, calls=%fused_computation | convolution fusion | flops 1614807040 | bytes 7094272 | tf_op jit(solution)/shard_map/hrgc,cl->hrgl/dot_general | solution.py:446
  57.1 0.8 convolution_bitcast_fusion
  58.9 1.0 %fusion.5 = f32[2,8,16,4096]{3,2,1,0:T(8,128)S(1)} fusion(s32[4096]{0:T(1024)S(1)} %get-tuple-element.65, bf16[1,8,16,256]{3,2,1,0:T(8,128)(2,1)S(1)} %get-tuple-element.56, bf16[1,8,16,256]{3,2,1,0:T(8,128)(2,1)S(1)} %get-tuple-element.55), kind=kOutput, calls=%fused_computation.6 | convolution fusion | flops 537985024 | bytes 4341760 | tf_op jit(solution)/shard_map/hrgl,cl->hrgc/dot_general | solution.py:467
  60.0 0.6 fusion.10
  60.9 0.9 reshape.332.outgoing
  63.3 0.8 copy.121.changed
  64.1 0.7 copy.120.started
  64.9 0.6 copy.119
  65.5 27.8 %shard_map.174 = (f32[64,4,128]{2,1,0:T(4,128)}, f32[1,128]{1,0:T(1,128)}, f32[32,128]{1,0:T(8,128)}) custom-call(f32[64,4,128]{2,1,0:T(4,128)} %reshape.332.outgoing, f32[8,4,52,128]{3,2,1,0:T(8,128)} %get-tuple-element.13.all_occupied, f32[4,52,128]{2,1,0:T(8,128)} %bitcast.148, f32[1,128]{1,0:T(1,128)} %pad_bitcast_fusion.curvature_row, ...), custom_call_target="tpu_custom_call" | custom-call | tf_op jit(solution)/shard_map/pallas_call | solution.py:327
  93.3 0.7 slice_bitcast_fusion.4
  94.2 0.7 fusion.51
  95.3 1.0 convolution_bitcast_fusion.5
  96.3 1.1 %reshape.336 = f32[128,2,2,64]{3,2,1,0:T(2,128)S(1)} reshape(f32[64,4,128]{2,1,0:T(4,128)} %get-tuple-element.15) | data formatting | bytes 262144 | tf_op jit(solution)/shard_map/reshape | solution.py:491
  97.9 0.7 copy.129
  98.6 0.7 copy.130
  99.3 0.7 copy.131
  (77 shorter events, 6.3 us)
Async XLA Ops:
  0.6 4.5 %copy-start.12 = (f32[2]{0:T(128)S(1)}, f32[2]{0:T(128)}, u32[]{:S(2)}) copy-start(f32[2]{0:T(128)} %param.19) | copy-start | bytes 28
  2.4 50.8 %copy-start.9 = (s32[3328]{0:T(1024)S(1)}, s32[3328]{0:T(1024)}, u32[]{:S(2)}) copy-start(s32[3328]{0:T(1024)} %param.23) | copy-start | bytes 39940
  54.2 2.2 %copy-start.8 = (f32[2,2,128,64,1,1,1]{2,3,1,0,4,6,5:T(8,128)S(1)}, f32[2,2,128,64,1,1,1]{2,3,1,0,4,6,5:T(8,128)}, u32[]{:S(2)}) copy-start(f32[2,2,128,64,1,1,1]{2,3,1,0,4,6,5:T(8,128)} %constant.157) | copy-start | bytes 393220
  56.1 0.9 copy-start.6
  56.2 1.7 %copy-start.7 = (f32[2,128,128]{2,1,0:T(8,128)S(1)}, f32[2,128,128]{2,1,0:T(8,128)}, u32[]{:S(2)}) copy-start(f32[2,128,128]{2,1,0:T(8,128)} %param.22) | copy-start | bytes 393220
  56.2 1.8 %copy-start.2 = (f32[2,2,64,128,1,1]{3,2,1,0,5,4:T(8,128)S(1)}, f32[2,2,64,128,1,1]{3,2,1,0,5,4:T(8,128)}, u32[]{:S(2)}) copy-start(f32[2,2,64,128,1,1]{3,2,1,0,5,4:T(8,128)} %constant.159) | copy-start | bytes 393220
  59.9 2.1 %copy-start.11 = (f32[1,128]{1,0:T(1,128)S(1)}, f32[1,128]{1,0:T(1,128)}, u32[]{:S(2)}) copy-start(f32[1,128]{1,0:T(1,128)} %get-tuple-element.11.norm_row) | copy-start | bytes 1540
  59.9 2.2 %copy-start.14 = (s32[16]{0:T(128)S(1)}, s32[16]{0:T(128)}, u32[]{:S(2)}) copy-start(s32[16]{0:T(128)} %param.21) | copy-start | bytes 196
  59.9 2.3 %copy-start.15 = (f32[16]{0:T(128)S(1)}, f32[16]{0:T(128)}, u32[]{:S(2)}) copy-start(f32[16]{0:T(128)} %param.20) | copy-start | bytes 196
  60.0 2.5 %copy-start.1 = (f32[2,2,52,128]{3,1,2,0:T(2,128)S(1)}, f32[2,2,52,128]{3,1,2,0:T(2,128)}, u32[]{:S(2)}) copy-start(f32[2,2,52,128]{3,1,2,0:T(2,128)} %param.16) | copy-start | bytes 319492
  60.0 2.5 %copy-start.4 = (f32[2,2,52,128]{3,1,2,0:T(2,128)S(1)}, f32[2,2,52,128]{3,1,2,0:T(2,128)}, u32[]{:S(2)}) copy-start(f32[2,2,52,128]{3,1,2,0:T(2,128)} %param.17) | copy-start | bytes 319492
  60.7 34.6 %copy-start = (f32[8,4,52,128]{3,2,1,0:T(8,128)S(1)}, f32[8,4,52,128]{3,2,1,0:T(8,128)}, u32[]{:S(2)}) copy-start(f32[8,4,52,128]{3,2,1,0:T(8,128)} %get-tuple-element.13.all_occupied) | copy-start | bytes 2555908
  62.0 35.4 %copy-start.5 = (f32[2,2,128,128,1]{3,2,1,0,4:T(8,128)S(1)}, f32[2,2,128,128,1]{3,2,1,0,4:T(8,128)}, u32[]{:S(2)}) copy-start(f32[2,2,128,128,1]{3,2,1,0,4:T(8,128)} %constant.160) | copy-start | bytes 786436
  62.0 35.7 %copy-start.3 = (f32[2,2,52,128]{3,1,2,0:T(2,128)S(1)}, f32[2,2,52,128]{3,1,2,0:T(2,128)}, u32[]{:S(2)}) copy-start(f32[2,2,52,128]{3,1,2,0:T(2,128)} %param.15) | copy-start | bytes 319492
  62.1 35.8 %copy-start.13 = (f32[2]{0:T(128)}, f32[2]{0:T(128)S(1)}, u32[]{:S(2)}) copy-start(f32[2]{0:T(128)S(1)} %get-tuple-element.80) | copy-start | bytes 28
  93.3 6.7 %copy-start.10 = (f32[32,128]{1,0:T(8,128)S(1)}, f32[32,128]{1,0:T(8,128)}, u32[]{:S(2)}) copy-start(f32[32,128]{1,0:T(8,128)} %get-tuple-element.16) | copy-start | bytes 49156

commit v6 on v5

--- a/solution.py
+++ b/solution.py
@@ -128,8 +128,6 @@
         value = mixed(field)
         for part in range(parts):
             both[:, field * parts + part, :] = value[part * owners : (part + 1) * owners]
-    smooth[...] = mixed(2)
-    former[...] = mixed(3)
     all_norms[me] = norm_row[...]
     both_here[me] = both[me]
     all_occupied[my_group] = occupied[...]
@@ -150,6 +148,8 @@
     norm_start()
     both_start()
     occ_start()
+    smooth[...] = mixed(2)
+    former[...] = mixed(3)
     norm_wait()
     totals = jnp.sum(all_norms[...], axis=0)
     total_row[...] = totals

time: 101 us -> 101 us (level)
  no operation moved by 1% of the time
where the time goes in v6:
time: 101 us
  Pallas kernels  74.1 us (73%)
  local copies, waits for them, and re-layouts  13 us (13%)
  matrix products  6.36 us (6%)
  other arithmetic  6.04 us (6%)
  between operations  1.09 us (1%)
    pallas_call x1, Pallas kernels, begin(): pl.pallas_call(functools.partial(begin_kernel, sizes), out_shape=[jax.Sha...  46.4 us
    pallas_call x1, Pallas kernels, finish(): pl.pallas_call(functools.partial(finish_kernel, sizes), out_shape=[jax.Sh...  27.8 us
    unnamed x39, local copies, waits for them, and re-layouts  3.1 us

profile of v6, /device:TPU:1, one launch (start us, length us, event | category | flops | bytes accessed | tf_op | source)
XLA Modules:
  0.0 100.6 jit_solution(609847637694418659)
XLA Ops:
  0.6 0.8 fusion.47
  1.5 0.8 broadcast_multiply_fusion
  2.4 1.2 %fusion.26 = (f32[2]{0:T(128)S(1)}, f32[2,1,2,52,128]{4,3,0,2,1:T(8,128)S(1)}, f32[2,2,52,128]{3,2,0,1:T(8,128)S(1)}, f32[2,1,2,52,128]{4,3,0,2,1:T(8,128)S(1)}, f32[2,1,2,52,128]{4,3,0,2,1:T(8,128)S(1)}) fusion(f32[2,2,52,128]{3,1,2,0:T(2,128)} %param.16, f32[2,52,128]{2,1,0:T(8,128)S(1)} %copy.109, f32[52,128]{1,0:T(8,128)S(1)} %fusion.37, ...), kind=kLoop, calls=%fused_computation.52 | loop fusion | flops 186366 | bytes 931848 | tf_op jit(solution)/shard_map/reduce_sum | solution.py:415
  3.7 0.9 pad.19.clone
  4.5 0.7 copy.113
  5.7 46.4 %shard_map.173 = (f32[2,12,4096]{2,1,0:T(8,128)}, f32[8,4,52,128]{3,2,1,0:T(8,128)}, f32[1,128]{1,0:T(1,128)}) custom-call(f32[2,4,128,128]{3,2,1,0:T(8,128)} %bitcast.143, f32[2,256,128]{2,1,0:T(8,128)} %constant.156.table, f32[1,128]{1,0:T(1,128)} %get-tuple-element.71.norm_row, f32[1,128]{1,0:T(1,128)} %get-tuple-element.70.old_row, f32[4,52,128]{2,1,0:T(8,128)} %bitcast.147), custom_call_target="tpu_custom_call" | custom-call | tf_op jit(solution)/shard_map/pallas_call | solution.py:195
  52.1 1.1 %reshape.329 = f32[24,4096]{1,0:T(8,128)S(1)} reshape(f32[2,12,4096]{2,1,0:T(8,128)} %get-tuple-element.12) | data formatting | bytes 786432 | tf_op jit(solution)/shard_map/reshape | solution.py:437
  53.5 0.6 broadcast_select_fusion.1
  54.2 1.9 %fusion = f32[2,24,16,256]{3,2,1,0:T(8,128)S(1)} fusion(bf16[1,24,16,4096]{3,2,1,0:T(8,128)(2,1)S(1)} %get-tuple-element.58, bf16[1,24,16,4096]{3,2,1,0:T(8,128)(2,1)S(1)} %get-tuple-element.57, s32[4096]{0:T(1024)S(1)} %get-tuple-element.65), kind=kOutput, calls=%fused_computation | convolution fusion | flops 1614807040 | bytes 7094272 | tf_op jit(solution)/shard_map/hrgc,cl->hrgl/dot_general | solution.py:446
  57.1 0.8 convolution_bitcast_fusion
  58.9 1.0 %fusion.5 = f32[2,8,16,4096]{3,2,1,0:T(8,128)S(1)} fusion(s32[4096]{0:T(1024)S(1)} %get-tuple-element.65, bf16[1,8,16,256]{3,2,1,0:T(8,128)(2,1)S(1)} %get-tuple-element.56, bf16[1,8,16,256]{3,2,1,0:T(8,128)(2,1)S(1)} %get-tuple-element.55), kind=kOutput, calls=%fused_computation.6 | convolution fusion | flops 537985024 | bytes 4341760 | tf_op jit(solution)/shard_map/hrgl,cl->hrgc/dot_general | solution.py:467
  60.0 0.6 fusion.10
  60.9 0.9 reshape.332.outgoing
  63.3 0.8 copy.121.changed
  64.1 0.7 copy.120.started
  64.9 0.6 copy.119
  65.5 27.8 %shard_map.174 = (f32[64,4,128]{2,1,0:T(4,128)}, f32[1,128]{1,0:T(1,128)}, f32[32,128]{1,0:T(8,128)}) custom-call(f32[64,4,128]{2,1,0:T(4,128)} %reshape.332.outgoing, f32[8,4,52,128]{3,2,1,0:T(8,128)} %get-tuple-element.13.all_occupied, f32[4,52,128]{2,1,0:T(8,128)} %bitcast.148, f32[1,128]{1,0:T(1,128)} %pad_bitcast_fusion.curvature_row, ...), custom_call_target="tpu_custom_call" | custom-call | tf_op jit(solution)/shard_map/pallas_call | solution.py:327
  93.3 0.7 slice_bitcast_fusion.4
  94.2 0.7 fusion.51
  95.3 1.0 convolution_bitcast_fusion.5
  96.3 1.1 %reshape.336 = f32[128,2,2,64]{3,2,1,0:T(2,128)S(1)} reshape(f32[64,4,128]{2,1,0:T(4,128)} %get-tuple-element.15) | data formatting | bytes 262144 | tf_op jit(solution)/shard_map/reshape | solution.py:491
  97.9 0.7 copy.129
  98.6 0.7 copy.130
  99.3 0.7 copy.131
  (77 shorter events, 6.3 us)
Async XLA Ops:
  0.6 4.5 %copy-start.12 = (f32[2]{0:T(128)S(1)}, f32[2]{0:T(128)}, u32[]{:S(2)}) copy-start(f32[2]{0:T(128)} %param.19) | copy-start | bytes 28
  2.4 50.8 %copy-start.9 = (s32[3328]{0:T(1024)S(1)}, s32[3328]{0:T(1024)}, u32[]{:S(2)}) copy-start(s32[3328]{0:T(1024)} %param.23) | copy-start | bytes 39940
  54.2 2.2 %copy-start.8 = (f32[2,2,128,64,1,1,1]{2,3,1,0,4,6,5:T(8,128)S(1)}, f32[2,2,128,64,1,1,1]{2,3,1,0,4,6,5:T(8,128)}, u32[]{:S(2)}) copy-start(f32[2,2,128,64,1,1,1]{2,3,1,0,4,6,5:T(8,128)} %constant.157) | copy-start | bytes 393220
  56.1 0.9 copy-start.6
  56.2 1.7 %copy-start.7 = (f32[2,128,128]{2,1,0:T(8,128)S(1)}, f32[2,128,128]{2,1,0:T(8,128)}, u32[]{:S(2)}) copy-start(f32[2,128,128]{2,1,0:T(8,128)} %param.22) | copy-start | bytes 393220
  56.2 1.8 %copy-start.2 = (f32[2,2,64,128,1,1]{3,2,1,0,5,4:T(8,128)S(1)}, f32[2,2,64,128,1,1]{3,2,1,0,5,4:T(8,128)}, u32[]{:S(2)}) copy-start(f32[2,2,64,128,1,1]{3,2,1,0,5,4:T(8,128)} %constant.159) | copy-start | bytes 393220
  59.9 2.1 %copy-start.11 = (f32[1,128]{1,0:T(1,128)S(1)}, f32[1,128]{1,0:T(1,128)}, u32[]{:S(2)}) copy-start(f32[1,128]{1,0:T(1,128)} %get-tuple-element.11.norm_row) | copy-start | bytes 1540
  59.9 2.2 %copy-start.14 = (s32[16]{0:T(128)S(1)}, s32[16]{0:T(128)}, u32[]{:S(2)}) copy-start(s32[16]{0:T(128)} %param.21) | copy-start | bytes 196
  59.9 2.3 %copy-start.15 = (f32[16]{0:T(128)S(1)}, f32[16]{0:T(128)}, u32[]{:S(2)}) copy-start(f32[16]{0:T(128)} %param.20) | copy-start | bytes 196
  60.0 2.5 %copy-start.1 = (f32[2,2,52,128]{3,1,2,0:T(2,128)S(1)}, f32[2,2,52,128]{3,1,2,0:T(2,128)}, u32[]{:S(2)}) copy-start(f32[2,2,52,128]{3,1,2,0:T(2,128)} %param.16) | copy-start | bytes 319492
  60.0 2.5 %copy-start.4 = (f32[2,2,52,128]{3,1,2,0:T(2,128)S(1)}, f32[2,2,52,128]{3,1,2,0:T(2,128)}, u32[]{:S(2)}) copy-start(f32[2,2,52,128]{3,1,2,0:T(2,128)} %param.17) | copy-start | bytes 319492
  60.7 34.6 %copy-start = (f32[8,4,52,128]{3,2,1,0:T(8,128)S(1)}, f32[8,4,52,128]{3,2,1,0:T(8,128)}, u32[]{:S(2)}) copy-start(f32[8,4,52,128]{3,2,1,0:T(8,128)} %get-tuple-element.13.all_occupied) | copy-start | bytes 2555908
  62.0 35.4 %copy-start.5 = (f32[2,2,128,128,1]{3,2,1,0,4:T(8,128)S(1)}, f32[2,2,128,128,1]{3,2,1,0,4:T(8,128)}, u32[]{:S(2)}) copy-start(f32[2,2,128,128,1]{3,2,1,0,4:T(8,128)} %constant.160) | copy-start | bytes 786436
  62.0 35.7 %copy-start.3 = (f32[2,2,52,128]{3,1,2,0:T(2,128)S(1)}, f32[2,2,52,128]{3,1,2,0:T(2,128)}, u32[]{:S(2)}) copy-start(f32[2,2,52,128]{3,1,2,0:T(2,128)} %param.15) | copy-start | bytes 319492
  62.1 35.8 %copy-start.13 = (f32[2]{0:T(128)}, f32[2]{0:T(128)S(1)}, u32[]{:S(2)}) copy-start(f32[2]{0:T(128)S(1)} %get-tuple-element.80) | copy-start | bytes 28
  93.3 6.7 %copy-start.10 = (f32[32,128]{1,0:T(8,128)S(1)}, f32[32,128]{1,0:T(8,128)}, u32[]{:S(2)}) copy-start(f32[32,128]{1,0:T(8,128)} %get-tuple-element.16) | copy-start | bytes 49156
